TPU v7x, 256 devices: a whole 4x4x8 slice. The times are simulated.
256 devices in a mesh: blk: 64 (over z_hi, y, x, core), grp: 4 (over z_lo).
Axes of the slice: x: 4, y: 4, z: 8 (z_hi: 2, z_lo: 4; z = z_hi * 4 + z_lo), core: 2. Of those that a mesh axis runs over, the one named last changes fastest.
Arguments:
- a_tiles: bfloat16 [2048, 64, 1024], P(('blk', 'grp')), may hold values from -0.75 to 0.75
- a_cols: int32 [2048, 16], P(('blk', 'grp')), may hold values from 0 to 2047, as said below
- p_tiles: bfloat16 [2048, 64, 256], P(('blk', 'grp')), may hold values from -0.75 to 0.75
- route_list: int32 [2048, 256], P(('blk', 'grp')), may hold values from 0 to 255, as said below
- out_slot: int32 [256, 256], P(('blk', 'grp')), may hold values from 0 to 127, as said below
Outputs:
- coarse_blocks: float32 [32768, 4096], P(('blk', 'grp'))
Inputs may be any that keep to these rules, and one draw needn't show every extreme that they name: `a_cols`: fine block row f is held by device f // 8 of blk+grp. Every entry in the rows of one device names a fine block row held by a device with the same grp index, and among the 128 entries of one device's rows exactly 2 name rows held by each blk index. `route_list`: A value o * 64 + p sends the partial block to send position p for the device with grp index o and the same blk index. For each device and each o, no position at or above a count is used, the count being at least 16, and 64 for one o of each device. `out_slot`: entry o * 64 + p of row d is the output block, among the 128 of the device with grp index o and the blk index of device d, into which send position p of device d adds; each output block index stands exactly 4 * 64 // 128 times in a row.
All inputs are finite; a program needn't handle non-finite values.
Results may differ from a plain program's by a relative error of at most 0.0029.
Values may be sent and summed in bfloat16 or wider, within the bound.
A program may use at most 128 MiB of HBM per device.

v0:
```python
import jax
import jax.numpy as jnp
from jax import lax
from jax.sharding import PartitionSpec as P

TILE = 64
RF = 8
KA = 16
KP = 4
CAP = 64
OSLOT = 128


def body(a_tiles, a_cols, p_tiles, route_list, out_slot):
    groups = lax.axis_size("grp")
    loop_len = lax.axis_size("blk")
    slot_count = RF * KA
    per_peer = slot_count // loop_len
    panel_width = KP * TILE
    a_blocks = a_tiles.reshape(RF, TILE, KA, TILE)
    flat_cols = a_cols.reshape(slot_count)
    holder = flat_cols // RF
    gathered_index = holder // groups * RF + flat_cols % RF
    ordering = jnp.argsort(gathered_index, stable=True)
    sorted_index = gathered_index[ordering]
    row_sorted = ordering // KA
    tile_sorted = ordering % KA
    initial = jnp.zeros((slot_count, TILE, panel_width), jnp.bfloat16)
    panel_piece = lax.all_gather(p_tiles, "blk", axis=0, tiled=True)
    offset = jnp.int32(0)
    piece_rows = panel_piece.shape[0]
    spanned = piece_rows // RF
    window = min(slot_count, per_peer * spanned)
    preceding = jnp.sum((sorted_index < offset).astype(jnp.int32))
    first_pos = jnp.minimum(preceding, slot_count - window)
    positions = first_pos + jnp.arange(window, dtype=jnp.int32)
    needed = sorted_index[positions]
    inside = (needed >= offset) & (needed < offset + piece_rows)
    local_rows = jnp.clip(needed, 0, piece_rows - 1)
    picked = a_blocks[row_sorted[positions], :, tile_sorted[positions], :]
    computed = jnp.einsum(
        "ats,aso->ato", picked, panel_piece[local_rows], preferred_element_type=jnp.float32
    ).astype(jnp.bfloat16)
    target = ordering[positions]
    previous = initial[target]
    y_slots = initial.at[target].set(jnp.where(inside[:, None, None], computed, previous))
    y_five = y_slots.reshape(RF, KA, TILE, KP, TILE)
    p_four = p_tiles.reshape(RF, TILE, KP, TILE)
    slot_row = out_slot[0]
    segment = route_list // CAP * OSLOT + slot_row[route_list]

    def accumulate(row_number, buffer):
        partials = jnp.einsum(
            "rsc,krqd->skqcd",
            p_four[row_number],
            y_five[row_number],
            preferred_element_type=jnp.float32,
        )
        return buffer.at[segment[row_number]].add(partials.reshape(KP * KA * KP, TILE * TILE))

    start_buffer = jnp.zeros((groups * OSLOT, TILE * TILE), jnp.float32)
    buffer = lax.fori_loop(0, RF, accumulate, start_buffer)
    result = lax.psum_scatter(buffer, "grp", scatter_dimension=0, tiled=True)
    return result


def solution(mesh):
    in_specs = (
        P(("blk", "grp"), None, None),
        P(("blk", "grp"), None),
        P(("blk", "grp"), None, None),
        P(("blk", "grp"), None),
        P(("blk", "grp"), None),
    )
    out_specs = P(("blk", "grp"), None)
    return jax.shard_map(body, mesh=mesh, in_specs=in_specs, out_specs=out_specs, check_vma=False)
```

profile of v0, /device:TPU:1, one launch (start us, length us, event | category | flops | bytes accessed | tf_op | source)
XLA Modules:
  0.0 659.4 jit_solution(12332405887019082903)
XLA Ops:
  23.9 13.2 %gather_fusion = s32[2048]{0:T(1024)S(1)} fusion(s32[256]{0:T(256)S(1)} %bitcast.57, s32[2048]{0:T(1024)S(1)} %broadcast_clamp_fusion), kind=kCustom, calls=%fused_computation | custom fusion | bytes 24576 | tf_op jit(solution)/shard_map/gather | solution.py:50
  46.9 121.7 %all-gather.2.cloned.1.call-done = bf16[512,64,256]{2,1,0:T(8,128)(2,1)} async-done(((bf16[8,64,256]{2,1,0:T(8,128)(2,1)}), bf16[512,64,256]{2,1,0:T(8,128)(2,1)}) %all-gather.2.cloned.1.call-update) | async-done | bytes 16777232 | tf_op jit(solution)/shard_map/all_gather | solution.py:29
  168.6 8.6 %gather_fusion.7 = bf16[128,64,256]{2,1,0:T(8,128)(2,1)} fusion(bf16[512,64,256]{2,1,0:T(8,128)(2,1)} %all-gather.2.cloned.1.call-done, s32[1024]{0:T(1024)S(1)} %pad_clamp_fusion.1), kind=kCustom, calls=%fused_computation.7 | custom fusion | bytes 8389120 | tf_op jit(solution)/shard_map/gather | solution.py:42
  183.9 19.3 %scatter_fusion.1 = bf16[128,64,256]{2,1,0:T(8,128)(2,1)} fusion(bf16[128,64,256]{2,1,0:T(8,128)(2,1)} %broadcast_in_dim.20, s32[128]{0:T(128)S(1)} %fusion.11, bf16[128,64,256]{2,1,0:T(8,128)(2,1)} %convert_select_fusion), kind=kCustom, calls=%fused_computation.10 | custom fusion | bytes 12583424 | tf_op jit(solution)/shard_map/scatter | solution.py:46
  203.2 8.4 %copy.19 = bf16[128,64,256]{1,2,0:T(8,128)(2,1)} copy(bf16[128,64,256]{2,1,0:T(8,128)(2,1)} %scatter_fusion.1) | data formatting | bytes 8388608 | tf_op jit(solution)/shard_map/while | solution.py:62
  215.8 290.8 %while.13 = (s32[]{:T(128)}, f32[512,4096]{1,0:T(8,128)}, s32[8,256]{1,0:T(8,128)S(1)}, bf16[8,16,64,4,64]{2,4,3,1,0:T(8,128)(2,1)}, bf16[8,64,4,64]{3,2,1,0:T(4,128)(2,1)S(1)}, /*index=5*/s32[]{:T(128)}) while((s32[]{:T(128)}, f32[512,4096]{1,0:T(8,128)}, s32[8,256]{1,0:T(8,128)S(1)}, bf16[8,16,64,4,64]{2,4,3,1,0:T(8,128)(2,1)}, ...), condition=%wide.region_5.6_spmd, body=%wide.region_3.5_spmd.sunk | while | flops 135267072 | bytes 34704972 | solution.py:62
  221.5 8.7 %copy.27 = f32[4,16,4,64,64]{4,3,2,1,0:T(8,128)} copy(f32[4,16,4,64,64]{3,4,0,2,1:T(8,128)} %convolution_bitcast_fusion.2) | data formatting | bytes 8388608 | tf_op jit(solution)/shard_map/while/body/eval_jaxpr/rsc,krqd->skqcd/transpose | solution.py:53
  230.3 7.9 %reshape.228 = f32[256,4096]{1,0:T(8,128)} reshape(f32[4,16,4,64,64]{4,3,2,1,0:T(8,128)} %copy.27) | data formatting | bytes 8388608 | tf_op jit(solution)/shard_map/while/body/eval_jaxpr/reshape | solution.py:59
  238.1 14.0 %scatter_fusion = f32[512,4096]{1,0:T(8,128)} fusion(f32[512,4096]{1,0:T(8,128)} %get-tuple-element.168, s32[256]{0:T(256)S(1)} %bitcast.59, f32[256,4096]{1,0:T(8,128)} %reshape.228), kind=kCustom, calls=%fused_computation.9.clone.1 | custom fusion | flops 1048576 | bytes 12583936 | tf_op jit(solution)/shard_map/while/body/eval_jaxpr/scatter-add | solution.py:59
  257.9 8.7 %copy.27 = f32[4,16,4,64,64]{4,3,2,1,0:T(8,128)} copy(f32[4,16,4,64,64]{3,4,0,2,1:T(8,128)} %convolution_bitcast_fusion.2) | data formatting | bytes 8388608 | tf_op jit(solution)/shard_map/while/body/eval_jaxpr/rsc,krqd->skqcd/transpose | solution.py:53
  274.5 14.0 %scatter_fusion = f32[512,4096]{1,0:T(8,128)} fusion(f32[512,4096]{1,0:T(8,128)} %get-tuple-element.168, s32[256]{0:T(256)S(1)} %bitcast.59, f32[256,4096]{1,0:T(8,128)} %reshape.228), kind=kCustom, calls=%fused_computation.9.clone.1 | custom fusion | flops 1048576 | bytes 12583936 | tf_op jit(solution)/shard_map/while/body/eval_jaxpr/scatter-add | solution.py:59
  294.2 8.7 %copy.27 = f32[4,16,4,64,64]{4,3,2,1,0:T(8,128)} copy(f32[4,16,4,64,64]{3,4,0,2,1:T(8,128)} %convolution_bitcast_fusion.2) | data formatting | bytes 8388608 | tf_op jit(solution)/shard_map/while/body/eval_jaxpr/rsc,krqd->skqcd/transpose | solution.py:53
  310.8 14.0 %scatter_fusion = f32[512,4096]{1,0:T(8,128)} fusion(f32[512,4096]{1,0:T(8,128)} %get-tuple-element.168, s32[256]{0:T(256)S(1)} %bitcast.59, f32[256,4096]{1,0:T(8,128)} %reshape.228), kind=kCustom, calls=%fused_computation.9.clone.1 | custom fusion | flops 1048576 | bytes 12583936 | tf_op jit(solution)/shard_map/while/body/eval_jaxpr/scatter-add | solution.py:59
  330.6 8.7 %copy.27 = f32[4,16,4,64,64]{4,3,2,1,0:T(8,128)} copy(f32[4,16,4,64,64]{3,4,0,2,1:T(8,128)} %convolution_bitcast_fusion.2) | data formatting | bytes 8388608 | tf_op jit(solution)/shard_map/while/body/eval_jaxpr/rsc,krqd->skqcd/transpose | solution.py:53
  347.2 14.0 %scatter_fusion = f32[512,4096]{1,0:T(8,128)} fusion(f32[512,4096]{1,0:T(8,128)} %get-tuple-element.168, s32[256]{0:T(256)S(1)} %bitcast.59, f32[256,4096]{1,0:T(8,128)} %reshape.228), kind=kCustom, calls=%fused_computation.9.clone.1 | custom fusion | flops 1048576 | bytes 12583936 | tf_op jit(solution)/shard_map/while/body/eval_jaxpr/scatter-add | solution.py:59
  366.9 8.7 %copy.27 = f32[4,16,4,64,64]{4,3,2,1,0:T(8,128)} copy(f32[4,16,4,64,64]{3,4,0,2,1:T(8,128)} %convolution_bitcast_fusion.2) | data formatting | bytes 8388608 | tf_op jit(solution)/shard_map/while/body/eval_jaxpr/rsc,krqd->skqcd/transpose | solution.py:53
  383.5 14.0 %scatter_fusion = f32[512,4096]{1,0:T(8,128)} fusion(f32[512,4096]{1,0:T(8,128)} %get-tuple-element.168, s32[256]{0:T(256)S(1)} %bitcast.59, f32[256,4096]{1,0:T(8,128)} %reshape.228), kind=kCustom, calls=%fused_computation.9.clone.1 | custom fusion | flops 1048576 | bytes 12583936 | tf_op jit(solution)/shard_map/while/body/eval_jaxpr/scatter-add | solution.py:59
  403.3 8.7 %copy.27 = f32[4,16,4,64,64]{4,3,2,1,0:T(8,128)} copy(f32[4,16,4,64,64]{3,4,0,2,1:T(8,128)} %convolution_bitcast_fusion.2) | data formatting | bytes 8388608 | tf_op jit(solution)/shard_map/while/body/eval_jaxpr/rsc,krqd->skqcd/transpose | solution.py:53
  419.9 14.0 %scatter_fusion = f32[512,4096]{1,0:T(8,128)} fusion(f32[512,4096]{1,0:T(8,128)} %get-tuple-element.168, s32[256]{0:T(256)S(1)} %bitcast.59, f32[256,4096]{1,0:T(8,128)} %reshape.228), kind=kCustom, calls=%fused_computation.9.clone.1 | custom fusion | flops 1048576 | bytes 12583936 | tf_op jit(solution)/shard_map/while/body/eval_jaxpr/scatter-add | solution.py:59
  439.6 8.7 %copy.27 = f32[4,16,4,64,64]{4,3,2,1,0:T(8,128)} copy(f32[4,16,4,64,64]{3,4,0,2,1:T(8,128)} %convolution_bitcast_fusion.2) | data formatting | bytes 8388608 | tf_op jit(solution)/shard_map/while/body/eval_jaxpr/rsc,krqd->skqcd/transpose | solution.py:53
  456.2 14.0 %scatter_fusion = f32[512,4096]{1,0:T(8,128)} fusion(f32[512,4096]{1,0:T(8,128)} %get-tuple-element.168, s32[256]{0:T(256)S(1)} %bitcast.59, f32[256,4096]{1,0:T(8,128)} %reshape.228), kind=kCustom, calls=%fused_computation.9.clone.1 | custom fusion | flops 1048576 | bytes 12583936 | tf_op jit(solution)/shard_map/while/body/eval_jaxpr/scatter-add | solution.py:59
  476.0 8.7 %copy.27 = f32[4,16,4,64,64]{4,3,2,1,0:T(8,128)} copy(f32[4,16,4,64,64]{3,4,0,2,1:T(8,128)} %convolution_bitcast_fusion.2) | data formatting | bytes 8388608 | tf_op jit(solution)/shard_map/while/body/eval_jaxpr/rsc,krqd->skqcd/transpose | solution.py:53
  492.6 14.0 %scatter_fusion = f32[512,4096]{1,0:T(8,128)} fusion(f32[512,4096]{1,0:T(8,128)} %get-tuple-element.168, s32[256]{0:T(256)S(1)} %bitcast.59, f32[256,4096]{1,0:T(8,128)} %reshape.228), kind=kCustom, calls=%fused_computation.9.clone.1 | custom fusion | flops 1048576 | bytes 12583936 | tf_op jit(solution)/shard_map/while/body/eval_jaxpr/scatter-add | solution.py:59
  506.7 145.9 %reduce-scatter.2.cloned.1.call-done = f32[128,4096]{1,0:T(8,128)} async-done(((f32[512,4096]{1,0:T(8,128)}), f32[128,4096]{1,0:T(8,128)}) %reduce-scatter.2.cloned.1.call-update) | async-done | bytes 2097168 | tf_op jit(solution)/shard_map/reduce_scatter | solution.py:63
  (78 shorter events, 138.1 us)
Async XLA Ops:
  6.5 17.4 %copy-start = (s32[1,256]{1,0:T(1,128)S(1)}, s32[1,256]{1,0:T(1,128)}, u32[]{:S(2)}) copy-start(s32[1,256]{1,0:T(1,128)} %param.11) | copy-start | bytes 3076
  6.5 12.9 %copy-start.3 = (bf16[8,64,1024]{2,1,0:T(8,128)(2,1)S(1)}, bf16[8,64,1024]{2,1,0:T(8,128)(2,1)}, u32[]{:S(2)}) copy-start(bf16[8,64,1024]{2,1,0:T(8,128)(2,1)} %param.7) | copy-start | bytes 3145732
  6.5 162.1 %all-gather.2.cloned.1.call-start = ((), (), s32[]{:S(2)}) async-start(), calls=%async_computation.1 | async-start | bytes 17039360 | tf_op jit(solution)/shard_map/all_gather | solution.py:29
  7.3 645.3 %reduce-scatter.2.cloned.1.call-start = ((), (), s32[]{:S(2)}) async-start(), calls=%async_computation.2 | async-start | bytes 10485760 | tf_op jit(solution)/shard_map/reduce_scatter | solution.py:63
  16.9 6.9 %copy-start.4 = (s32[8,256]{1,0:T(8,128)S(1)}, s32[8,256]{1,0:T(8,128)}, u32[]{:S(2)}) copy-start(s32[8,256]{1,0:T(8,128)} %param.10) | copy-start | bytes 24580
  46.9 130.2 %copy-start.2 = (bf16[128,64,64]{2,1,0:T(8,128)(2,1)S(1)}, bf16[128,64,64]{2,1,0:T(8,128)(2,1)}, u32[]{:S(2)}) copy-start(bf16[128,64,64]{2,1,0:T(8,128)(2,1)} %gather_fusion.6) | copy-start | bytes 3145732
  506.6 145.9 %copy-start.1 = (s32[1,256]{1,0:T(1,128)S(1)}, s32[1,256]{1,0:T(1,128)}, u32[]{:S(2)}) copy-start(s32[1,256]{1,0:T(1,128)} %param.11) | copy-start | bytes 3076
Sparse Core Ops, SparseCore 0:
  10.9 157.6 all-gather.1
  506.8 145.7 reduce-scatter.1
where the time goes:
time: 663 us; the launch traced here: 659 us
  waiting for transfers between devices  268 us (40%)
  local copies, waits for them, and re-layouts  209 us (32%)
  other arithmetic  116 us (17%)
  matrix products  52.1 us (8%)
  between operations  14.2 us (2%)
    reduce_scatter x1, waiting for transfers between devices, body(): result = lax.psum_scatter(buffer, 'grp', scatter_dimension=0, tiled=True)  146 us
    all_gather x1, waiting for transfers between devices, body(): panel_piece = lax.all_gather(p_tiles, 'blk', axis=0, tiled=True)  122 us
    scatter-add x8, other arithmetic, accumulate(): buffer.at[segment[row_number]]  112 us
    transpose x8, local copies, waits for them, and re-layouts, accumulate(): jnp.einsum('rsc,krqd->skqcd', p_four[row_number], y_five[row_number], pre...  69.8 us
    reshape x8, local copies, waits for them, and re-layouts, accumulate(): partials.reshape(KP * KA * KP, TILE * TILE)  63.1 us
    dot_general x8, matrix products, accumulate(): jnp.einsum('rsc,krqd->skqcd', p_four[row_number], y_five[row_number], pre...  45.3 us
    scatter x1, local copies, waits for them, and re-layouts, body(): initial.at[target].set(jnp.where(inside[:, None, None], computed, previous))  19.3 us
  transfers between devices with their start and end apart: 2, of which 2 were waited for; matrix products, arithmetic and copies ran while one was open for 6% of the time, Pallas kernels for 0%

commit v1 on v0

v1 whole, which is shorter than its diff:
```python
import heapq

import jax
import jax.numpy as jnp
from jax import lax
from jax.experimental import pallas as pl
from jax.experimental.pallas import tpu as pltpu
from jax.sharding import PartitionSpec as P

TILE = 64
RF = 8
KA = 16
KP = 4
CAP = 64
OSLOT = 128
GRP = 4
SLOTS = RF * KA
POS = GRP * CAP
MESH = pl.DeviceIdType.MESH
NACC = 4


def low_lanes(shape):
    return lax.broadcasted_iota(jnp.int32, shape, 1) < TILE


def turned(block):
    return pltpu.roll(block.astype(jnp.float32), TILE, 1).astype(jnp.bfloat16)


def product_kernel(cols_ref, route_ref, me_ref, a_ref, p_ref, panel_ref, send_ref, own_ref, picked, weights, *rest):
    accs, sems = rest[:NACC], rest[NACC]

    @pl.loop(0, SLOTS)
    def _(m):
        i = m // KA
        pltpu.make_async_copy(panel_ref.at[cols_ref[m]], picked.at[m], sems.at[i]).start()

    @pl.loop(0, POS)
    def _(r):
        for acc in accs:
            acc[r] = jnp.zeros((32, 128), jnp.float32)

    low = low_lanes((TILE, 128))
    zero = jnp.zeros((TILE, 128), jnp.bfloat16)

    @pl.loop(0, RF)
    def _(i):
        pltpu.make_async_copy(panel_ref.at[pl.ds(0, KA)], picked.at[pl.ds(i * KA, KA)], sems.at[i]).wait()
        for half in range(2):
            pair = p_ref[i, :, half * 128:(half + 1) * 128]
            back = turned(pair)
            even, odd = 2 * half * 128, (2 * half + 1) * 128
            weights[0:TILE, even:even + 128] = jnp.where(low, pair, zero)
            weights[TILE:128, even:even + 128] = jnp.where(low, zero, back)
            weights[0:TILE, odd:odd + 128] = jnp.where(low, back, zero)
            weights[TILE:128, odd:odd + 128] = jnp.where(low, zero, pair)

        @pl.loop(0, KA // 2)
        def _(kk):
            pair = a_ref[i, :, pl.ds(pl.multiple_of(kk * 128, 128), 128)]
            back = turned(pair)
            for parity in range(2):
                first, second = (pair, back) if parity == 0 else (back, pair)
                tile = jnp.concatenate([jnp.where(low, first, zero), jnp.where(low, zero, second)], axis=0)
                k = kk * 2 + parity
                y = lax.dot_general(
                    picked[i * KA + k], tile, (((1,), (1,)), ((), ())), preferred_element_type=jnp.float32
                ).astype(jnp.bfloat16)
                for s in range(KP):
                    w = jnp.dot(y, weights[:, s * 128:(s + 1) * 128], preferred_element_type=jnp.float32)
                    for q in range(KP):
                        r = route_ref[i * 256 + (s * KA + k) * KP + q]
                        acc = accs[(s * KP + q) % NACC]
                        acc[r] = acc[r] + w[q * 32:(q + 1) * 32]

    @pl.loop(0, POS)
    def _(r):
        total = accs[0][r]
        for acc in accs[1:]:
            total = total + acc[r]
        send_ref[r] = total.astype(jnp.bfloat16)

    @pl.loop(0, CAP)
    def _(p):
        r = me_ref[0] * CAP + p
        total = accs[0][r]
        for acc in accs[1:]:
            total = total + acc[r]
        own_ref[p] = total


def product(cols, route, me, a_tiles, p_tiles, panel):
    smem = pl.BlockSpec(memory_space=pltpu.SMEM)
    vmem = pl.BlockSpec(memory_space=pltpu.VMEM)
    return pl.pallas_call(
        product_kernel,
        out_shape=(
            jax.ShapeDtypeStruct((POS, 32, 128), jnp.bfloat16),
            jax.ShapeDtypeStruct((CAP, 32, 128), jnp.float32),
        ),
        in_specs=[smem, smem, smem, vmem, vmem, pl.BlockSpec(memory_space=pl.ANY)],
        out_specs=(vmem, vmem),
        scratch_shapes=[
            pltpu.VMEM((SLOTS, 128, 128), jnp.bfloat16),
            pltpu.VMEM((128, 512), jnp.bfloat16),
        ]
        + [pltpu.VMEM((POS, 32, 128), jnp.float32)] * NACC
        + [pltpu.SemaphoreType.DMA((RF,))],
        compiler_params=pltpu.CompilerParams(vmem_limit_bytes=48 * 1024 * 1024),
        name="product",
    )(cols, route, me, a_tiles, p_tiles, panel)


def exchange_kernel(send_ref, slot_ref, recv_ref, rslot_ref, send_sems, recv_sems, slot_send, slot_recv):
    blk, me = lax.axis_index("blk"), lax.axis_index("grp")
    barrier = pltpu.get_barrier_semaphore()

    def partner(j):
        flip_low = me + 1 - 2 * lax.rem(me, 2)
        if j == 1:
            return flip_low
        flip_high = lax.rem(me + 2, 4)
        if j == 2:
            return flip_high
        return 3 - me

    for j in (1, 2, 3):
        pl.semaphore_signal(barrier, inc=1, device_id=(blk, partner(j)), device_id_type=MESH)
    pl.semaphore_wait(barrier, 3)
    copies = []
    for j in (3, 2, 1):
        other = partner(j)
        copies.append(pltpu.make_async_remote_copy(
            src_ref=slot_ref, dst_ref=rslot_ref.at[j - 1], send_sem=slot_send.at[j - 1], recv_sem=slot_recv.at[j - 1],
            device_id=(blk, other), device_id_type=MESH))
        copies.append(pltpu.make_async_remote_copy(
            src_ref=send_ref.at[pl.ds(other * CAP, CAP)], dst_ref=recv_ref.at[j - 1],
            send_sem=send_sems.at[j - 1], recv_sem=recv_sems.at[j - 1], device_id=(blk, other), device_id_type=MESH))
    for copy in copies:
        copy.start()
    for copy in copies:
        copy.wait()


def exchange(send, slots):
    anywhere = pl.BlockSpec(memory_space=pl.ANY)
    return pl.pallas_call(
        exchange_kernel,
        out_shape=(
            jax.ShapeDtypeStruct((3, CAP, 32, 128), jnp.bfloat16),
            jax.ShapeDtypeStruct((3, 2, 128), jnp.int32),
        ),
        in_specs=[anywhere, anywhere],
        out_specs=(anywhere, anywhere),
        scratch_shapes=[pltpu.SemaphoreType.DMA((3,))] * 4,
        compiler_params=pltpu.CompilerParams(collective_id=1, has_side_effects=True),
        name="exchange",
    )(send, slots)


def collect_kernel(slot_ref, rslot_ref, me_ref, own_ref, recv_ref, out_ref, acc, flipped):
    me = me_ref[0]

    @pl.loop(0, OSLOT)
    def _(b):
        acc[b] = jnp.zeros((32, 128), jnp.float32)

    @pl.loop(0, CAP)
    def _(p):
        b = slot_ref[me * CAP + p]
        acc[b] = acc[b] + own_ref[p]

    for j in range(3):
        @pl.loop(0, CAP)
        def _(p):
            b = rslot_ref[j * POS + me * CAP + p]
            acc[b] = acc[b] + recv_ref[j, p].astype(jnp.float32)

    lane = lax.broadcasted_iota(jnp.int32, (32, 128), 1)
    low = lane < 64
    even = lax.rem(lane // 32, 2) == 0

    @pl.loop(0, OSLOT // 8)
    def _(g):
        for quad in range(2):
            block = acc[pl.ds(g * 8 + quad * 4, 4)].reshape(128, 128)
            flipped[quad] = block.T
            parts = [
                flipped[quad, pl.ds(half * 64 + parity, 32, stride=2), :]
                for parity in range(2) for half in range(2)
            ]
            mid = [None] * 4
            for n in range(2):
                a, b = parts[n], parts[n + 2]
                mid[n] = jnp.where(low, a, pltpu.roll(b, 64, 1))
                mid[n + 2] = jnp.where(low, pltpu.roll(a, 64, 1), b)
            for n in range(2):
                a, b = mid[2 * n], mid[2 * n + 1]
                first = jnp.where(even, a, pltpu.roll(b, 32, 1))
                second = jnp.where(even, pltpu.roll(a, 96, 1), b)
                for which, value in ((2 * n, first), (2 * n + 1, second)):
                    out_ref[pl.ds(g * 256 + quad * 4 + which, 32, stride=8), :] = value


def collect(slots, rslots, me, own, recv):
    smem = pl.BlockSpec(memory_space=pltpu.SMEM)
    vmem = pl.BlockSpec(memory_space=pltpu.VMEM)
    return pl.pallas_call(
        collect_kernel,
        out_shape=jax.ShapeDtypeStruct((OSLOT * 32, 128), jnp.float32),
        in_specs=[smem, smem, smem, vmem, vmem],
        out_specs=vmem,
        scratch_shapes=[pltpu.VMEM((OSLOT, 32, 128), jnp.float32), pltpu.VMEM((2, 128, 128), jnp.float32)],
        compiler_params=pltpu.CompilerParams(vmem_limit_bytes=32 * 1024 * 1024),
        name="collect",
    )(slots, rslots, me, own, recv)


NBLK = 64
STEPS = (0, 1, -1, 2)
PIECES = [
    (layer, first, turn, along, across)
    for layer in (0, 1) for first in (0, 1) for turn in (0, 1) for along in STEPS for across in STEPS
]
PIECE_ID = {piece: number for number, piece in enumerate(PIECES)}


def next_hops(piece):
    layer, first, turn, along, across = piece
    dims = ("x", "y") if first == 0 else ("y", "x")
    sign = 1 - 2 * turn
    hops = []
    if across == 0:
        if along == 0:
            hops += [(dims[0], sign, (layer, first, turn, 1, 0)), (dims[0], -sign, (layer, first, turn, -1, 0))]
        if along == 1:
            hops += [(dims[0], sign, (layer, first, turn, 2, 0))]
        hops += [(dims[1], sign, (layer, first, turn, along, 1)), (dims[1], -sign, (layer, first, turn, along, -1))]
    elif across == 1:
        hops += [(dims[1], sign, (layer, first, turn, along, 2))]
    return hops


def arrival_order(slot=1.46, latency=2.0, far_slot=5.8, far_latency=4.0, issue=0.05):
    heap, order, free, clock, count = [], [], {}, 0.0, 0
    for layer in (0, 1):
        for number, (first, turn) in enumerate(((0, 0), (0, 1), (1, 0), (1, 1))):
            when = 0.0 if layer == 0 else (number + 1) * far_slot + far_latency
            heapq.heappush(heap, (when, 0, count, (layer, first, turn, 0, 0)))
            count += 1
    while heap:
        when, _, _, piece = heapq.heappop(heap)
        clock = max(clock, when)
        order.append(piece)
        for dim, sign, after in next_hops(piece):
            clock += issue
            free[dim, sign] = max(clock, free.get((dim, sign), 0.0)) + slot
            heapq.heappush(heap, (free[dim, sign] + latency, -len(next_hops(after)), count, after))
            count += 1
        clock += issue
    return order


def gather_kernel(own_ref, panel_ref, send_sem, recv_sems, near_send, near_recv, own_sem):
    blk, grp = lax.axis_index("blk"), lax.axis_index("grp")
    core = lax.rem(blk, 2)
    x = lax.rem(blk // 2, 4)
    y = lax.rem(blk // 8, 4)
    high = blk // 32
    where = {"x": x, "y": y}

    def number(high, y, x, core):
        return ((high * 4 + y) * 4 + x) * 2 + core

    def moved(dim, by):
        at = dict(where)
        at[dim] = lax.rem(at[dim] + by + 4, 4)
        return number(high, at["y"], at["x"], core)

    sibling = number(high, y, x, 1 - core)
    opposite = number(1 - high, y, x, core)
    neighbours = {(dim, sign): moved(dim, sign) for dim in ("x", "y") for sign in (1, -1)}

    barrier = pltpu.get_barrier_semaphore()
    for other in (sibling, opposite, *neighbours.values()):
        pl.semaphore_signal(barrier, inc=1, device_id=(other, grp), device_id_type=MESH)
    pl.semaphore_wait(barrier, 6)

    def origin(piece):
        layer, first, turn, along, across = piece
        sign = 1 - 2 * turn
        dims = ("x", "y") if first == 0 else ("y", "x")
        at = dict(where)
        at[dims[0]] = lax.rem(at[dims[0]] - sign * along + 4, 4)
        at[dims[1]] = lax.rem(at[dims[1]] - sign * across + 4, 4)
        return number(high if layer == 0 else 1 - high, at["y"], at["x"], core)

    def rows(piece):
        return pl.ds(2 * (2 * piece[1] + piece[2]), 2)

    def remote(src, dst, sems, target):
        return pltpu.make_async_remote_copy(
            src_ref=src, dst_ref=dst, send_sem=sems[0], recv_sem=sems[1], device_id=(target, grp), device_id_type=MESH)

    def held(piece):
        return panel_ref.at[origin(piece), rows(piece)]

    mine = pltpu.make_async_copy(own_ref, panel_ref.at[blk], own_sem.at[0])
    for piece in ORDER[:4]:
        for dim, sign, after in next_hops(piece):
            remote(own_ref.at[rows(piece)], held(piece), (send_sem.at[0], recv_sems.at[PIECE_ID[after]]),
                   neighbours[dim, sign]).start()
        far = (1,) + piece[1:]
        remote(own_ref.at[rows(piece)], held(piece), (send_sem.at[0], recv_sems.at[PIECE_ID[far]]), opposite).start()
    remote(own_ref, panel_ref.at[blk], (near_send.at[0], near_recv.at[0]), sibling).start()
    mine.start()
    for piece in ORDER[4:]:
        here = held(piece)
        remote(here, here, (send_sem.at[0], recv_sems.at[PIECE_ID[piece]]), sibling).wait_recv()
        for dim, sign, after in next_hops(piece):
            remote(here, here, (send_sem.at[0], recv_sems.at[PIECE_ID[after]]), neighbours[dim, sign]).start()
        remote(here, here, (near_send.at[0], near_recv.at[0]), sibling).start()
    mine.wait()
    most = panel_ref.at[pl.ds(0, 31)]
    pltpu.make_async_copy(most, most, send_sem.at[0]).wait()
    half = panel_ref.at[pl.ds(0, 32)]
    pltpu.make_async_copy(half, half, near_send.at[0]).wait()
    pltpu.make_async_copy(half, half, near_recv.at[0]).wait()


ORDER = arrival_order()


def gather(own):
    anywhere = pl.BlockSpec(memory_space=pl.ANY)
    return pl.pallas_call(
        gather_kernel,
        out_shape=jax.ShapeDtypeStruct((NBLK, RF, 128, 128), jnp.bfloat16),
        in_specs=[anywhere],
        out_specs=anywhere,
        scratch_shapes=[
            pltpu.SemaphoreType.DMA((1,)),
            pltpu.SemaphoreType.DMA((len(PIECES),)),
            pltpu.SemaphoreType.DMA((1,)),
            pltpu.SemaphoreType.DMA((1,)),
            pltpu.SemaphoreType.DMA((1,)),
        ],
        compiler_params=pltpu.CompilerParams(collective_id=0, has_side_effects=True),
        name="gather",
    )(own)


def arranged(p_tiles):
    return p_tiles.reshape(RF, TILE, KP, 2, 32).transpose(0, 2, 4, 3, 1).reshape(RF, 128, 128)


def body(a_tiles, a_cols, p_tiles, route_list, out_slot):
    me = lax.axis_index("grp").astype(jnp.int32).reshape(1)
    cols = a_cols.reshape(SLOTS)
    cols = cols // (RF * GRP) * RF + cols % RF
    panel = gather(arranged(p_tiles)).reshape(NBLK * RF, 128, 128)
    send, own = product(cols, route_list.reshape(RF * 256), me, a_tiles, p_tiles, panel)
    slots = out_slot.reshape(2, 128)
    recv, rslots = exchange(send, slots)
    out = collect(slots.reshape(POS), rslots.reshape(3 * POS), me, own, recv)
    return out.reshape(16, 32, 8, 128).transpose(0, 2, 1, 3).reshape(OSLOT, TILE * TILE)


def solution(mesh):
    in_specs = (
        P(("blk", "grp"), None, None),
        P(("blk", "grp"), None),
        P(("blk", "grp"), None, None),
        P(("blk", "grp"), None),
        P(("blk", "grp"), None),
    )
    out_specs = P(("blk", "grp"), None)
    return jax.shard_map(body, mesh=mesh, in_specs=in_specs, out_specs=out_specs, check_vma=False)
```

time: 663 us -> 179 us (0.27)
  waiting for transfers between devices: 268 us -> 0 us
  local copies, waits for them, and re-layouts: 209 us -> 7.58 us
  Pallas kernels: 0 us -> 171 us
  other arithmetic: 116 us -> 0.01 us
  matrix products: 52.1 us -> 0 us
  between operations: 14.2 us -> 0.07 us
    pallas_call x0 -> x4, Pallas kernels: none -> 171 us  [the longest x1 71.5 us: gather(): pl.pallas_call(gather_kernel, out_shape=jax.ShapeDtypeStruct((NBLK, RF, 1...]
    reduce_scatter x1 -> x0, waiting for transfers between devices: 146 us -> none  [body(): result = lax.psum_scatter(buffer, 'grp', scatter_dimension=0, tiled=True)]
    all_gather x1 -> x0, waiting for transfers between devices: 122 us -> none  [body(): panel_piece = lax.all_gather(p_tiles, 'blk', axis=0, tiled=True)]
    scatter-add x8 -> x0, other arithmetic: 112 us -> none  [accumulate(): buffer.at[segment[row_number]]]
    transpose x8 -> x1, local copies, waits for them, and re-layouts: 69.8 us -> 0.52 us  [arranged(): p_tiles.reshape(RF, TILE, KP, 2, 32).transpose(0, 2, 4, 3, 1)]
    reshape x12 -> x3, local copies, waits for them, and re-layouts: 69.5 us -> 2.41 us  [the longest x1 0.96 us: arranged(): p_tiles.reshape(RF, TILE, KP, 2, 32).transpose(0, 2, 4, 3, 1)]
    dot_general x9 -> x0, matrix products: 52.1 us -> none  [the longest x8 45.3 us: accumulate(): jnp.einsum('rsc,krqd->skqcd', p_four[row_number], y_five[row_number], pre...]
    gather x10 -> x0, local copies, waits for them, and re-layouts: 35.1 us -> none  [the longest x2 13.2 us: body(): segment = route_list // CAP * OSLOT + slot_row[route_list]]
  transfers between devices with their start and end apart: 2 -> 0, of which waited for: 2 -> 0; matrix products, arithmetic and copies ran while one was open for 6% -> 0% of each run, Pallas kernels for 0% -> 0%
where the time goes in v1:
time: 179 us
  Pallas kernels  171 us (96%)
  local copies, waits for them, and re-layouts  7.58 us (4%)
    pallas_call x1, Pallas kernels, gather(): pl.pallas_call(gather_kernel, out_shape=jax.ShapeDtypeStruct((NBLK, RF, 1...  71.5 us
    pallas_call x1, Pallas kernels, exchange(): pl.pallas_call(exchange_kernel, out_shape=(jax.ShapeDtypeStruct((3, CAP,...  48.5 us
    pallas_call x1, Pallas kernels, product(): pl.pallas_call(product_kernel, out_shape=(jax.ShapeDtypeStruct((POS, 32,...  42.4 us
    pallas_call x1, Pallas kernels, collect(): pl.pallas_call(collect_kernel, out_shape=jax.ShapeDtypeStruct((OSLOT * 32...  8.96 us
    unnamed x12, local copies, waits for them, and re-layouts  4.66 us

profile of v1, /device:TPU:1, one launch (start us, length us, event | category | flops | bytes accessed | tf_op | source)
XLA Modules:
  0.0 179.0 jit_solution(1204676645762396036)
XLA Ops:
  0.0 0.8 reshape.30
  0.8 0.7 copy.9
  1.5 1.2 copy.7
  2.7 0.5 copy.8
  3.2 1.0 reshape.34.own_ref
  4.2 0.0 copy-start.2
  4.2 0.0 copy-start.3
  4.2 71.5 %gather.1 = bf16[64,8,128,128]{3,2,1,0:T(8,128)(2,1)} custom-call(bf16[8,128,128]{2,1,0:T(8,128)(2,1)} %reshape.34.own_ref), custom_call_target="tpu_custom_call" | custom-call | tf_op jit(solution)/shard_map/gather/pallas_call | solution.py:337
  75.7 0.0 copy-done.2
  75.7 0.0 copy-done.3
  75.7 42.4 %product.1 = (bf16[256,32,128]{2,1,0:T(8,128)(2,1)S(1)}, f32[64,32,128]{2,1,0:T(8,128)S(1)}) custom-call(s32[128]{0:T(128)S(1)} %fusion.cols_ref, s32[2048]{0:T(1024)S(1)} %bitcast.16, s32[1]{0:T(128)} %bitcast.1.me_ref, bf16[8,64,1024]{2,1,0:T(8,128)(2,1)S(1)} %copy-done.3, bf16[8,64,256]{2,1,0:T(8,128)(2,1)S(1)} %copy-done.2, bf16[512,128,128]{2,1,0:T(8,128)(2,1)} %bitcast.19), custom_call_target="tpu_custom_call" | custom-call | tf_op jit(solution)/shard_map/product/pallas_call | solution.py:96
  118.2 0.0 copy-start
  118.2 1.3 copy-done
  119.5 0.0 copy-start.4
  119.5 48.5 %exchange.1 = (bf16[3,64,32,128]{3,2,1,0:T(8,128)(2,1)}, s32[3,2,128]{2,1,0:T(2,128)}) custom-call(bf16[256,32,128]{2,1,0:T(8,128)(2,1)} %copy-done, s32[2,128]{1,0:T(2,128)} %bitcast.17), custom_call_target="tpu_custom_call" | custom-call | tf_op jit(solution)/shard_map/exchange/pallas_call | solution.py:148
  167.9 0.7 reshape.37.rslot_ref
  168.6 0.0 copy-done.4
  168.6 0.0 copy-start.1
  168.6 1.4 copy-done.1
  170.0 9.0 %collect.1 = f32[4096,128]{1,0:T(8,128)} custom-call(s32[256]{0:T(256)S(1)} %bitcast.18, s32[768]{0:T(1024)S(1)} %reshape.37.rslot_ref, s32[1]{0:T(128)} %bitcast.1.me_ref, f32[64,32,128]{2,1,0:T(8,128)S(1)} %get-tuple-element.11.own_ref, bf16[3,64,32,128]{3,2,1,0:T(8,128)(2,1)S(1)} %copy-done.1), custom_call_target="tpu_custom_call" | custom-call | tf_op jit(solution)/shard_map/collect/pallas_call | solution.py:209
  (1 shorter events, 0.0 us)
Async XLA Ops:
  4.2 71.5 %copy-start.2 = (bf16[8,64,256]{2,1,0:T(8,128)(2,1)S(1)}, bf16[8,64,256]{2,1,0:T(8,128)(2,1)}, u32[]{:S(2)}) copy-start(bf16[8,64,256]{2,1,0:T(8,128)(2,1)} %p_ref.1) | copy-start | bytes 786436
  4.2 71.5 %copy-start.3 = (bf16[8,64,1024]{2,1,0:T(8,128)(2,1)S(1)}, bf16[8,64,1024]{2,1,0:T(8,128)(2,1)}, u32[]{:S(2)}) copy-start(bf16[8,64,1024]{2,1,0:T(8,128)(2,1)} %a_ref.1) | copy-start | bytes 3145732
  118.2 1.3 copy-start
  119.5 49.1 %copy-start.4 = (s32[1,256]{1,0:T(1,128)S(1)}, s32[1,256]{1,0:T(1,128)}, u32[]{:S(2)}) copy-start(s32[1,256]{1,0:T(1,128)} %param.9) | copy-start | bytes 3076
  168.6 1.4 copy-start.1

commit v2 on v1

v2 whole, which is shorter than its diff:
```python
import heapq

import jax
import jax.numpy as jnp
from jax import lax
from jax.experimental import pallas as pl
from jax.experimental.pallas import tpu as pltpu
from jax.sharding import PartitionSpec as P

TILE = 64
RF = 8
KA = 16
KP = 4
CAP = 64
OSLOT = 128
GRP = 4
SLOTS = RF * KA
POS = GRP * CAP
MESH = pl.DeviceIdType.MESH
NACC = 4
LOW = 16
ROWS = KP * LOW
YUN = 8
WUN = 8


def low_lanes(shape):
    return lax.broadcasted_iota(jnp.int32, shape, 1) < TILE


def turned(block):
    return pltpu.roll(block.astype(jnp.float32), TILE, 1).astype(jnp.bfloat16)


def product_kernel(cols_ref, route_ref, me_ref, tiles_ref, p_ref, panel_ref, send_ref, own_ref, weights, ys, a_ref, a_sem,
                   *accs):
    fetch = pltpu.make_async_copy(tiles_ref, a_ref, a_sem.at[0])
    fetch.start()
    low = low_lanes((TILE, 128))
    zero = jnp.zeros((TILE, 128), jnp.bfloat16)

    @pl.loop(0, RF)
    def _(i):
        for half in range(2):
            pair = p_ref[i, :, half * 128:(half + 1) * 128]
            back = turned(pair)
            even, odd = 2 * half * 128, (2 * half + 1) * 128
            weights[i, 0:TILE, even:even + 128] = jnp.where(low, pair, zero)
            weights[i, TILE:128, even:even + 128] = jnp.where(low, zero, back)
            weights[i, 0:TILE, odd:odd + 128] = jnp.where(low, back, zero)
            weights[i, TILE:128, odd:odd + 128] = jnp.where(low, zero, pair)

    @pl.loop(0, POS // 4)
    def _(r):
        for acc in accs:
            acc[pl.ds(pl.multiple_of(r * 4 * LOW, 8), 4 * LOW), :] = jnp.zeros((4 * LOW, 128), jnp.float32)

    fetch.wait()

    @pl.loop(0, RF)
    def _(i):
        @pl.loop(0, KA // YUN)
        def _(kk):
            for u in range(YUN // 2):
                pair = a_ref[i, :, pl.ds(pl.multiple_of(kk * (64 * YUN) + u * 128, 128), 128)]
                back = turned(pair)
                for parity in range(2):
                    first, second = (pair, back) if parity == 0 else (back, pair)
                    tile = jnp.concatenate([jnp.where(low, first, zero), jnp.where(low, zero, second)], axis=0)
                    m = i * KA + kk * YUN + 2 * u + parity
                    ys[m] = lax.dot_general(
                        panel_ref[cols_ref[m]], tile, (((1,), (1,)), ((), ())), preferred_element_type=jnp.float32
                    ).astype(jnp.bfloat16)

    @pl.loop(0, SLOTS // WUN)
    def _(step):
        i = step // (KA // WUN)
        k0 = lax.rem(step, KA // WUN) * WUN
        base = i * 256 + k0 * KP
        y = ys[pl.ds(step * WUN, WUN)].reshape(WUN * ROWS, 128)
        w = [
            jnp.dot(y, weights[i, :, sp * 256:(sp + 1) * 256], preferred_element_type=jnp.float32)
            for sp in range(2)
        ]
        for u in range(WUN):
            for q in range(KP):
                for s in range(KP):
                    r = route_ref[base + (s * KA + u) * KP + q]
                    acc = accs[s % NACC]
                    row, lane = u * ROWS + q * LOW, s % 2 * 128
                    here = pl.ds(pl.multiple_of(r, LOW), LOW)
                    acc[here, :] = acc[here, :] + w[s // 2][row:row + LOW, lane:lane + 128]

    def total(r, count):
        here = pl.ds(pl.multiple_of(r * LOW, LOW), count * LOW)
        value = (accs[0][here, :] + accs[1][here, :]) + (accs[2][here, :] + accs[3][here, :])
        return value.reshape(count, LOW, 128)

    @pl.loop(0, POS // 4)
    def _(step):
        send_ref[pl.ds(step * 4, 4)] = total(step * 4, 4).astype(jnp.bfloat16)

    @pl.loop(0, CAP // 4)
    def _(step):
        own_ref[pl.ds(step * 4, 4)] = total(me_ref[0] * CAP + step * 4, 4)


def product(cols, route, me, a_tiles, p_tiles, panel):
    smem = pl.BlockSpec(memory_space=pltpu.SMEM)
    vmem = pl.BlockSpec(memory_space=pltpu.VMEM)
    return pl.pallas_call(
        product_kernel,
        out_shape=(
            jax.ShapeDtypeStruct((POS, LOW, 128), jnp.bfloat16),
            jax.ShapeDtypeStruct((CAP, LOW, 128), jnp.float32),
        ),
        in_specs=[smem, smem, smem, pl.BlockSpec(memory_space=pltpu.HBM), vmem, vmem],
        out_specs=(vmem, vmem),
        scratch_shapes=[
            pltpu.VMEM((RF, 128, 512), jnp.bfloat16),
            pltpu.VMEM((SLOTS, ROWS, 128), jnp.bfloat16),
            pltpu.VMEM((RF, TILE, KA * TILE), jnp.bfloat16),
            pltpu.SemaphoreType.DMA((1,)),
        ]
        + [pltpu.VMEM((POS * LOW, 128), jnp.float32)] * NACC,
        compiler_params=pltpu.CompilerParams(vmem_limit_bytes=16 * 1024 * 1024),
        name="product",
    )(cols, route, me, a_tiles, p_tiles, panel)


def collect_kernel(slot_ref, rslot_ref, me_ref, own0_ref, own1_ref, recv0_ref, recv1_ref, out_ref, *scratch):
    accs, flipped = scratch[:4], scratch[4]
    me = me_ref[0]

    @pl.loop(0, OSLOT // 2)
    def _(b):
        for acc in accs:
            acc[pl.ds(b * 2, 2)] = jnp.zeros((2, 32, 128), jnp.float32)

    @pl.loop(0, CAP // 2)
    def _(step):
        for e in range(2):
            p = step * 2 + e
            for j in range(4):
                b = slot_ref[me * CAP + p] if j == 3 else rslot_ref[j * POS + me * CAP + p]
                low = own0_ref[p] if j == 3 else recv0_ref[j, p].astype(jnp.float32)
                high = own1_ref[p] if j == 3 else recv1_ref[j, p].astype(jnp.float32)
                accs[j][b, 0:LOW] = accs[j][b, 0:LOW] + low
                accs[j][b, LOW:] = accs[j][b, LOW:] + high

    lane = lax.broadcasted_iota(jnp.int32, (32, 128), 1)
    low = lane < 64
    even = lax.rem(lane // 32, 2) == 0

    @pl.loop(0, OSLOT // 8)
    def _(g):
        for quad in range(2):
            here = pl.ds(g * 8 + quad * 4, 4)
            block = ((accs[0][here] + accs[1][here]) + (accs[2][here] + accs[3][here])).reshape(128, 128)
            flipped[quad] = block.T
            parts = [
                flipped[quad, pl.ds(half * 64 + parity, 32, stride=2), :]
                for parity in range(2) for half in range(2)
            ]
            mid = [None] * 4
            for n in range(2):
                a, b = parts[n], parts[n + 2]
                mid[n] = jnp.where(low, a, pltpu.roll(b, 64, 1))
                mid[n + 2] = jnp.where(low, pltpu.roll(a, 64, 1), b)
            for n in range(2):
                a, b = mid[2 * n], mid[2 * n + 1]
                first = jnp.where(even, a, pltpu.roll(b, 32, 1))
                second = jnp.where(even, pltpu.roll(a, 96, 1), b)
                for which, value in ((2 * n, first), (2 * n + 1, second)):
                    out_ref[pl.ds(g * 256 + quad * 4 + which, 32, stride=8), :] = value


def collect(slots, rslots, me, own0, own1, recv0, recv1):
    smem = pl.BlockSpec(memory_space=pltpu.SMEM)
    vmem = pl.BlockSpec(memory_space=pltpu.VMEM)
    return pl.pallas_call(
        collect_kernel,
        out_shape=jax.ShapeDtypeStruct((OSLOT * 32, 128), jnp.float32),
        in_specs=[smem, smem, smem, vmem, vmem, vmem, vmem],
        out_specs=vmem,
        scratch_shapes=[pltpu.VMEM((OSLOT, 32, 128), jnp.float32)] * 4 + [pltpu.VMEM((2, 128, 128), jnp.float32)],
        compiler_params=pltpu.CompilerParams(vmem_limit_bytes=16 * 1024 * 1024),
        name="collect",
    )(slots, rslots, me, own0, own1, recv0, recv1)


NBLK = 64
STEPS = (0, 1, -1, 2)
PIECES = [
    (layer, first, turn, along, across)
    for layer in (0, 1) for first in (0, 1) for turn in (0, 1) for along in STEPS for across in STEPS
]
PIECE_ID = {piece: number for number, piece in enumerate(PIECES)}


def next_hops(piece):
    layer, first, turn, along, across = piece
    dims = ("x", "y") if first == 0 else ("y", "x")
    sign = 1 - 2 * turn
    hops = []
    if across == 0:
        if along == 0:
            hops += [(dims[0], sign, (layer, first, turn, 1, 0)), (dims[0], -sign, (layer, first, turn, -1, 0))]
        if along == 1:
            hops += [(dims[0], sign, (layer, first, turn, 2, 0))]
        hops += [(dims[1], sign, (layer, first, turn, along, 1)), (dims[1], -sign, (layer, first, turn, along, -1))]
    elif across == 1:
        hops += [(dims[1], sign, (layer, first, turn, along, 2))]
    return hops


def arrival_order(slot=1.46, latency=2.0, far_slot=5.8, far_latency=4.0, issue=0.05):
    heap, order, free, clock, count = [], [], {}, 0.0, 0
    for layer in (0, 1):
        for number, (first, turn) in enumerate(((0, 0), (0, 1), (1, 0), (1, 1))):
            when = 0.0 if layer == 0 else (number + 1) * far_slot + far_latency
            heapq.heappush(heap, (when, 0, count, (layer, first, turn, 0, 0)))
            count += 1
    while heap:
        when, _, _, piece = heapq.heappop(heap)
        clock = max(clock, when)
        order.append(piece)
        for dim, sign, after in next_hops(piece):
            clock += issue
            free[dim, sign] = max(clock, free.get((dim, sign), 0.0)) + slot
            heapq.heappush(heap, (free[dim, sign] + latency, -len(next_hops(after)), count, after))
            count += 1
        clock += issue
    return order


def remote(src, dst, send_sem, recv_sem, target):
    return pltpu.make_async_remote_copy(
        src_ref=src, dst_ref=dst, send_sem=send_sem, recv_sem=recv_sem, device_id=target, device_id_type=MESH)


def partners():
    blk, me = lax.axis_index("blk"), lax.axis_index("grp")
    return {1: (blk, me + 1 - 2 * lax.rem(me, 2)), 2: (blk, lax.rem(me + 2, 4)), 3: (blk, 3 - me)}


class Place:
    def __init__(self):
        self.blk, self.grp = lax.axis_index("blk"), lax.axis_index("grp")
        self.core = lax.rem(self.blk, 2)
        self.at = {"x": lax.rem(self.blk // 2, 4), "y": lax.rem(self.blk // 8, 4)}
        self.high = self.blk // 32
        self.sibling = (self.number(self.high, self.at, 1 - self.core), self.grp)
        self.far = self.number(1 - self.high, self.at, self.core)
        self.opposite = (self.far, self.grp)
        self.neighbours = {
            (dim, sign): (self.moved(dim, sign), self.grp) for dim in ("x", "y") for sign in (1, -1)
        }

    def number(self, high, at, core):
        return ((high * 4 + at["y"]) * 4 + at["x"]) * 2 + core

    def moved(self, dim, by):
        at = dict(self.at)
        at[dim] = lax.rem(at[dim] + by + 4, 4)
        return self.number(self.high, at, self.core)

    def origin(self, piece):
        layer, first, turn, along, across = piece
        sign = 1 - 2 * turn
        dims = ("x", "y") if first == 0 else ("y", "x")
        at = dict(self.at)
        at[dims[0]] = lax.rem(at[dims[0]] - sign * along + 4, 4)
        at[dims[1]] = lax.rem(at[dims[1]] - sign * across + 4, 4)
        return self.number(self.high if layer == 0 else 1 - self.high, at, self.core)


def greet(targets):
    barrier = pltpu.get_barrier_semaphore()
    for target in targets:
        pl.semaphore_signal(barrier, inc=1, device_id=target, device_id_type=MESH)
    pl.semaphore_wait(barrier, len(targets))


def rows(piece):
    return pl.ds(2 * (2 * piece[1] + piece[2]), 2)


def settle(ref, count, sem):
    part = ref.at[pl.ds(0, count)]
    pltpu.make_async_copy(part, part, sem).wait()


def spread(place, panel_ref, order, start, sems, between):
    send_sem, recv_sems, near_send, near_recv = sems

    def held(piece):
        return panel_ref.at[place.origin(piece), rows(piece)]

    for piece in start:
        source = start[piece]
        for dim, sign, after in next_hops(piece):
            remote(source, held(piece), send_sem.at[0], recv_sems.at[PIECE_ID[after]], place.neighbours[dim, sign]).start()
    count = 0
    for piece in order:
        if piece in start:
            continue
        if count in between:
            between[count]()
        count += 1
        here = held(piece)
        remote(here, here, send_sem.at[0], recv_sems.at[PIECE_ID[piece]], place.sibling).wait_recv()
        for dim, sign, after in next_hops(piece):
            remote(here, here, send_sem.at[0], recv_sems.at[PIECE_ID[after]], place.neighbours[dim, sign]).start()
        remote(here, here, near_send.at[0], near_recv.at[0], place.sibling).start()


ORIGINS = [(first, turn, 0, 0) for first, turn in ((0, 0), (0, 1), (1, 0), (1, 1))]


def gather_kernel(own_ref, panel_ref, later_ref, send_sem, recv_sems, near_send, near_recv, first_sems, later_sems,
                  own_sem, transit, later_transit):
    place = Place()
    z = place.high * 4 + place.grp

    def above(by):
        level = lax.rem(z + by + 8, 8)
        return place.number(level // 4, place.at, place.core), lax.rem(level, 4)

    greet([place.sibling, above(1), above(-1), above(3), above(-3), *place.neighbours.values()])
    start = {(0,) + piece: own_ref.at[0, rows((0,) + piece)] for piece in ORIGINS}
    sems = (send_sem, recv_sems, near_send, near_recv)
    lates = []

    def first_leg():
        for number, piece in enumerate(start):
            remote(start[piece], transit.at[number], send_sem.at[0], first_sems.at[number],
                   above(1 - 2 * piece[2])).start()
        for turn in range(2):
            part = pl.ds(4 * turn, 4)
            lates.append(remote(own_ref.at[1, part], later_transit.at[turn], later_sems.at[turn], later_sems.at[2 + turn],
                                above(1 - 2 * turn)))
            lates[-1].start()
        remote(own_ref.at[0], panel_ref.at[place.blk], near_send.at[0], near_recv.at[0], place.sibling).start()
        pltpu.make_async_copy(own_ref.at[0], panel_ref.at[place.blk], own_sem.at[0]).start()
        for number, piece in enumerate(start):
            up = 1 - 2 * piece[2]
            remote(transit.at[number], transit.at[number], send_sem.at[0], first_sems.at[number], above(up)).wait_recv()
            remote(transit.at[number], panel_ref.at[above(-up)[0], rows(piece)], send_sem.at[0],
                   recv_sems.at[PIECE_ID[(1,) + piece[1:]]], above(3 * up)).start()

    def second_leg():
        for turn in range(2):
            lates[turn].wait_recv()
            lates.append(remote(later_transit.at[turn], later_ref.at[pl.ds(4 * turn, 4)], later_sems.at[4 + turn],
                                later_sems.at[6 + turn], above(3 * (1 - 2 * turn))))
            lates[-1].start()

    spread(place, panel_ref, ORDER_A, start, sems, {0: first_leg, 24: second_leg})
    pltpu.make_async_copy(own_ref.at[0], panel_ref.at[place.blk], own_sem.at[0]).wait()
    for turn in range(2):
        lates[turn].wait_send()
        lates[2 + turn].wait()
    settle(panel_ref, 32, send_sem.at[0])
    settle(panel_ref, 32, near_send.at[0])
    settle(panel_ref, 32, near_recv.at[0])


def swap(send_ref, recv_ref, sems):
    send_sems, recv_sems = sems
    copies = []
    for j, target in reversed(partners().items()):
        copies.append(remote(
            send_ref.at[pl.ds(target[1] * CAP, CAP)], recv_ref.at[j - 1], send_sems.at[j - 1], recv_sems.at[j - 1],
            target))
        copies[-1].start()
    return copies


def gather_swap_kernel(own_ref, later_ref, send_ref, slot_ref, panel_ref, recv_ref, rslot_ref, send_sem, recv_sems,
                       near_send, near_recv, own_sems, swap_send, swap_recv, slot_send, slot_recv):
    place = Place()
    greet([place.sibling, *place.neighbours.values(), *partners().values()])
    copies = swap(send_ref, recv_ref, (swap_send, swap_recv))
    start = {(0,) + piece: own_ref.at[1, rows((0,) + piece)] for piece in ORIGINS}
    start |= {(1,) + piece: later_ref.at[rows((1,) + piece)] for piece in ORIGINS}
    mine = []

    def rest():
        for number, (source, slot) in enumerate(((own_ref.at[1], place.blk), (later_ref, place.far))):
            remote(source, panel_ref.at[slot], near_send.at[0], near_recv.at[0], place.sibling).start()
            mine.append(pltpu.make_async_copy(source, panel_ref.at[slot], own_sems.at[number]))
            mine[-1].start()
        for j, target in partners().items():
            copies.append(remote(slot_ref, rslot_ref.at[j - 1], slot_send.at[j - 1], slot_recv.at[j - 1], target))
            copies[-1].start()

    spread(place, panel_ref, ORDER_B, start, (send_sem, recv_sems, near_send, near_recv), {0: rest})
    for copy in mine:
        copy.wait()
    settle(panel_ref, 30, send_sem.at[0])
    settle(panel_ref, 32, near_send.at[0])
    settle(panel_ref, 32, near_recv.at[0])
    for copy in copies:
        copy.wait()


def swap_kernel(send_ref, recv_ref, swap_send, swap_recv):
    greet(list(partners().values()))
    for copy in swap(send_ref, recv_ref, (swap_send, swap_recv)):
        copy.wait()


ORDER_A = arrival_order(slot=0.73, far_slot=1.5, far_latency=5.0)
ORDER_B = arrival_order(slot=0.73, far_slot=0.0, far_latency=0.0)
ANYWHERE = pl.BlockSpec(memory_space=pl.ANY)
PANEL = jax.ShapeDtypeStruct((NBLK, RF, ROWS, 128), jnp.bfloat16)
RECV = jax.ShapeDtypeStruct((3, CAP, LOW, 128), jnp.bfloat16)
ONE = pltpu.SemaphoreType.DMA((1,))
TWO = pltpu.SemaphoreType.DMA((2,))
THREE = pltpu.SemaphoreType.DMA((3,))
MANY = pltpu.SemaphoreType.DMA((len(PIECES),))


def gather(own):
    return pl.pallas_call(
        gather_kernel,
        out_shape=(PANEL, jax.ShapeDtypeStruct((RF, ROWS, 128), jnp.bfloat16)),
        in_specs=[ANYWHERE],
        out_specs=(ANYWHERE, ANYWHERE),
        scratch_shapes=[
            ONE, MANY, ONE, ONE, pltpu.SemaphoreType.DMA((4,)), pltpu.SemaphoreType.DMA((8,)), ONE,
            pltpu.VMEM((4, 2, ROWS, 128), jnp.bfloat16),
            pltpu.VMEM((2, 4, ROWS, 128), jnp.bfloat16),
        ],
        compiler_params=pltpu.CompilerParams(collective_id=0, has_side_effects=True, vmem_limit_bytes=1 << 20),
        cost_estimate=pl.CostEstimate(flops=0, transcendentals=0, bytes_accessed=1 << 26),
        name="gather",
    )(own)


def gather_swap(own, later, send, slots):
    return pl.pallas_call(
        gather_swap_kernel,
        out_shape=(PANEL, RECV, jax.ShapeDtypeStruct((3, 2, 128), jnp.int32)),
        in_specs=[ANYWHERE] * 4,
        out_specs=(ANYWHERE, ANYWHERE, ANYWHERE),
        scratch_shapes=[ONE, MANY, ONE, ONE, TWO, THREE, THREE, THREE, THREE],
        compiler_params=pltpu.CompilerParams(collective_id=1, has_side_effects=True, vmem_limit_bytes=1 << 20),
        cost_estimate=pl.CostEstimate(flops=0, transcendentals=0, bytes_accessed=1 << 26),
        name="gather_swap",
    )(own, later, send, slots)


def exchange(send):
    return pl.pallas_call(
        swap_kernel,
        out_shape=RECV,
        in_specs=[ANYWHERE],
        out_specs=ANYWHERE,
        scratch_shapes=[THREE, THREE],
        compiler_params=pltpu.CompilerParams(collective_id=2, has_side_effects=True, vmem_limit_bytes=1 << 20),
        name="exchange",
    )(send)


def arrange_kernel(p_ref, out_ref):
    group = lax.broadcasted_iota(jnp.int32, (TILE, 128), 1) // 32

    def merged(parts):
        value = parts[0]
        for number in (1, 2, 3):
            value = jnp.where(group == number, parts[number], value)
        return value

    @pl.loop(0, RF)
    def _(i):
        left = p_ref[i, :, 0:128].astype(jnp.float32)
        right = p_ref[i, :, 128:256].astype(jnp.float32)
        first = merged([left, pltpu.roll(left, 96, 1), pltpu.roll(right, 64, 1), pltpu.roll(right, 32, 1)])
        second = merged([pltpu.roll(left, 96, 1), pltpu.roll(left, 64, 1), pltpu.roll(right, 32, 1), right])
        block = jnp.concatenate([first, second], axis=0).T.astype(jnp.bfloat16)
        for q in range(KP):
            for part in range(2):
                out_ref[part, i, q * LOW:(q + 1) * LOW, :] = block[q * 32 + part * LOW:q * 32 + (part + 1) * LOW]


def arranged(p_tiles):
    vmem = pl.BlockSpec(memory_space=pltpu.VMEM)
    return pl.pallas_call(
        arrange_kernel,
        out_shape=jax.ShapeDtypeStruct((2, RF, ROWS, 128), jnp.bfloat16),
        in_specs=[vmem],
        out_specs=vmem,
        compiler_params=pltpu.CompilerParams(vmem_limit_bytes=4 * 1024 * 1024),
        name="arrange",
    )(p_tiles)


def body(a_tiles, a_cols, p_tiles, route_list, out_slot):
    me = lax.axis_index("grp").astype(jnp.int32).reshape(1)
    cols = a_cols.reshape(SLOTS)
    cols = cols // (RF * GRP) * RF + cols % RF
    route = route_list.reshape(RF * 256) * LOW
    slots = out_slot.reshape(2, 128)
    arranged_tiles = arranged(p_tiles)
    panel0, later = gather(arranged_tiles)
    send0, own0 = product(cols, route, me, a_tiles, p_tiles, panel0.reshape(NBLK * RF, ROWS, 128))
    panel1, recv0, rslots = gather_swap(arranged_tiles, later, send0, slots)
    send1, own1 = product(cols, route, me, a_tiles, p_tiles, panel1.reshape(NBLK * RF, ROWS, 128))
    recv1 = exchange(send1)
    out = collect(slots.reshape(POS), rslots.reshape(3 * POS), me, own0, own1, recv0, recv1)
    return out.reshape(16, 32, 8, 128).transpose(0, 2, 1, 3).reshape(OSLOT, TILE * TILE)


def solution(mesh):
    in_specs = (
        P(("blk", "grp"), None, None),
        P(("blk", "grp"), None),
        P(("blk", "grp"), None, None),
        P(("blk", "grp"), None),
        P(("blk", "grp"), None),
    )
    out_specs = P(("blk", "grp"), None)
    return jax.shard_map(body, mesh=mesh, in_specs=in_specs, out_specs=out_specs, check_vma=False)
```

time: 179 us -> 139 us (0.78)
  Pallas kernels: 171 us -> 134 us
  local copies, waits for them, and re-layouts: 7.58 us -> 3.92 us
    pallas_call x3 -> x6, Pallas kernels: 162 us -> 126 us  [the longest x1 42.4 us: gather(): pl.pallas_call(gather_kernel, out_shape=(PANEL, jax.ShapeDtypeStruct((RF,...]
    unnamed x12 -> x11, local copies, waits for them, and re-layouts: 4.66 us -> 3.13 us
where the time goes in v2:
time: 139 us; the launch traced here: 138 us
  Pallas kernels  134 us (96%)
  local copies, waits for them, and re-layouts  3.92 us (3%)
    pallas_call x1, Pallas kernels, gather(): pl.pallas_call(gather_kernel, out_shape=(PANEL, jax.ShapeDtypeStruct((RF,...  42.4 us
    pallas_call x1, Pallas kernels, gather_swap(): pl.pallas_call(gather_swap_kernel, out_shape=(PANEL, RECV, jax.ShapeDtype...  30 us
    pallas_call x2, Pallas kernels, product(): pl.pallas_call(product_kernel, out_shape=(jax.ShapeDtypeStruct((POS, LOW,...  26.6 us
    pallas_call x1, Pallas kernels, exchange(): pl.pallas_call(swap_kernel, out_shape=RECV, in_specs=[ANYWHERE], out_spec...  25.7 us
    pallas_call x1, Pallas kernels, collect(): pl.pallas_call(collect_kernel, out_shape=jax.ShapeDtypeStruct((OSLOT * 32...  7.58 us
    unnamed x11, local copies, waits for them, and re-layouts  3.13 us

profile of v2, /device:TPU:1, one launch (start us, length us, event | category | flops | bytes accessed | tf_op | source)
XLA Modules:
  0.0 138.4 jit_solution(3330596365338198917)
XLA Ops:
  0.0 0.0 copy-start.4
  0.0 0.8 reshape.27
  0.8 0.7 multiply_bitcast_fusion
  1.5 0.0 copy-start.2
  1.5 0.9 copy-done.2
  2.5 1.4 %arrange.1.own_ref = bf16[2,8,64,128]{3,2,1,0:T(8,128)(2,1)S(1)} custom-call(bf16[8,64,256]{2,1,0:T(8,128)(2,1)S(1)} %copy-done.2), custom_call_target="tpu_custom_call" | custom-call | tf_op jit(solution)/shard_map/arrange/pallas_call | solution.py:490
  3.9 42.4 %gather.1 = (bf16[64,8,64,128]{3,2,1,0:T(8,128)(2,1)S(1)}, bf16[8,64,128]{2,1,0:T(8,128)(2,1)S(1)}) custom-call(bf16[2,8,64,128]{3,2,1,0:T(8,128)(2,1)S(1)} %arrange.1.own_ref), custom_call_target="tpu_custom_call" | custom-call | bytes 67108864 | tf_op jit(solution)/shard_map/gather/pallas_call | solution.py:426
  46.3 0.0 copy-start
  46.3 1.2 copy-done
  47.5 0.0 copy-start.3
  47.5 0.9 copy-done.3
  48.4 0.0 copy-start.1
  48.4 13.3 %product.2 = (bf16[256,16,128]{2,1,0:T(8,128)(2,1)S(1)}, f32[64,16,128]{2,1,0:T(8,128)S(1)}) custom-call(s32[128]{0:T(128)S(1)} %fusion.cols_ref, s32[2048]{0:T(1024)S(1)} %bitcast.17, s32[1]{0:T(128)} %bitcast.1.me_ref, bf16[8,64,1024]{2,1,0:T(8,128)(2,1)S(1)} %copy-done, bf16[8,64,256]{2,1,0:T(8,128)(2,1)S(1)} %copy-done.3, bf16[512,64,128]{2,1,0:T(8,128)(2,1)S(1)} %bitcast.16), custom_call_target="tpu_custom_call" | custom-call | tf_op jit(solution)/shard_map/product/pallas_call | solution.py:111
  61.7 0.0 copy-done.4
  61.8 30.0 %gather_swap.1 = (bf16[64,8,64,128]{3,2,1,0:T(8,128)(2,1)S(1)}, bf16[3,64,16,128]{3,2,1,0:T(8,128)(2,1)S(1)}, s32[3,2,128]{2,1,0:T(2,128)S(1)}) custom-call(bf16[2,8,64,128]{3,2,1,0:T(8,128)(2,1)S(1)} %arrange.1.own_ref, bf16[8,64,128]{2,1,0:T(8,128)(2,1)S(1)} %get-tuple-element.14.later_ref, bf16[256,16,128]{2,1,0:T(8,128)(2,1)S(1)} %get-tuple-element.16.send_ref, ...), custom_call_target="tpu_custom_call" | custom-call | bytes 67108864 | tf_op jit(solution)/shard_map/gather_swap/pallas_call | solution.py:443
  91.7 0.0 copy-done.1
  91.8 13.3 %product.3 = (bf16[256,16,128]{2,1,0:T(8,128)(2,1)S(1)}, f32[64,16,128]{2,1,0:T(8,128)S(1)}) custom-call(s32[128]{0:T(128)S(1)} %fusion.cols_ref, s32[2048]{0:T(1024)S(1)} %bitcast.18, s32[1]{0:T(128)} %bitcast.1.me_ref, bf16[8,64,1024]{2,1,0:T(8,128)(2,1)S(1)} %copy-done.1, bf16[8,64,256]{2,1,0:T(8,128)(2,1)S(1)} %copy-done.3, ...), custom_call_target="tpu_custom_call" | custom-call | tf_op jit(solution)/shard_map/product/pallas_call | solution.py:111
  105.1 25.7 %exchange.1.recv1_ref = bf16[3,64,16,128]{3,2,1,0:T(8,128)(2,1)S(1)} custom-call(bf16[256,16,128]{2,1,0:T(8,128)(2,1)S(1)} %get-tuple-element.22.send_ref), custom_call_target="tpu_custom_call" | custom-call | tf_op jit(solution)/shard_map/exchange/pallas_call | solution.py:456
  130.8 7.6 %collect.1 = f32[4096,128]{1,0:T(8,128)} custom-call(s32[256]{0:T(256)S(1)} %bitcast.20, s32[768]{0:T(1024)S(1)} %reshape.31.rslot_ref, s32[1]{0:T(128)} %bitcast.1.me_ref, f32[64,16,128]{2,1,0:T(8,128)S(1)} %get-tuple-element.18.own0_ref, f32[64,16,128]{2,1,0:T(8,128)S(1)} %get-tuple-element.20.own1_ref, ...), custom_call_target="tpu_custom_call" | custom-call | tf_op jit(solution)/shard_map/collect/pallas_call | solution.py:181
  (3 shorter events, 0.0 us)
Async XLA Ops:
  0.0 61.7 %copy-start.4 = (s32[1,256]{1,0:T(1,128)S(1)}, s32[1,256]{1,0:T(1,128)}, u32[]{:S(2)}) copy-start(s32[1,256]{1,0:T(1,128)} %param.9) | copy-start | bytes 3076
  1.5 0.9 copy-start.2
  46.3 1.2 copy-start
  47.5 0.9 copy-start.3
  48.4 43.3 %copy-start.1 = (bf16[8,64,1024]{2,1,0:T(8,128)(2,1)S(1)}, bf16[8,64,1024]{2,1,0:T(8,128)(2,1)}, u32[]{:S(2)}) copy-start(bf16[8,64,1024]{2,1,0:T(8,128)(2,1)} %tiles_ref.3) | copy-start | bytes 3145732

commit v3 on v2

--- a/solution.py
+++ b/solution.py
@@ -1,3 +1,4 @@
+import functools
 import heapq
 
 import jax
@@ -20,8 +21,7 @@
 NACC = 4
 LOW = 16
 ROWS = KP * LOW
-YUN = 8
-WUN = 8
+WUN = 16
 
 
 def low_lanes(shape):
@@ -32,10 +32,7 @@
     return pltpu.roll(block.astype(jnp.float32), TILE, 1).astype(jnp.bfloat16)
 
 
-def product_kernel(cols_ref, route_ref, me_ref, tiles_ref, p_ref, panel_ref, send_ref, own_ref, weights, ys, a_ref, a_sem,
-                   *accs):
-    fetch = pltpu.make_async_copy(tiles_ref, a_ref, a_sem.at[0])
-    fetch.start()
+def build_weights(p_ref, weights):
     low = low_lanes((TILE, 128))
     zero = jnp.zeros((TILE, 128), jnp.bfloat16)
 
@@ -50,27 +47,34 @@
             weights[i, 0:TILE, odd:odd + 128] = jnp.where(low, back, zero)
             weights[i, TILE:128, odd:odd + 128] = jnp.where(low, zero, pair)
 
-    @pl.loop(0, POS // 4)
-    def _(r):
-        for acc in accs:
-            acc[pl.ds(pl.multiple_of(r * 4 * LOW, 8), 4 * LOW), :] = jnp.zeros((4 * LOW, 128), jnp.float32)
-
-    fetch.wait()
+
+def build_tiles(a_ref, tiles_ref, i):
+    low = low_lanes((TILE, 128))
+    zero = jnp.zeros((TILE, 128), jnp.bfloat16)
+
+    @pl.loop(0, KA // 2)
+    def _(kk):
+        pair = a_ref[i, :, pl.ds(pl.multiple_of(kk * 128, 128), 128)]
+        back = turned(pair)
+        for parity in range(2):
+            first, second = (pair, back) if parity == 0 else (back, pair)
+            m = i * KA + kk * 2 + parity
+            tiles_ref[m, 0:TILE, :] = jnp.where(low, first, zero)
+            tiles_ref[m, TILE:128, :] = jnp.where(low, zero, second)
+
+
+def product_kernel(cols_ref, route_ref, me_ref, tiles_ref, weights, panel_ref, blank0, blank1, blank2, blank3, send_ref,
+                   own_ref, acc0, acc1, acc2, acc3, ys):
+    accs = (acc0, acc1, acc2, acc3)
 
     @pl.loop(0, RF)
     def _(i):
-        @pl.loop(0, KA // YUN)
-        def _(kk):
-            for u in range(YUN // 2):
-                pair = a_ref[i, :, pl.ds(pl.multiple_of(kk * (64 * YUN) + u * 128, 128), 128)]
-                back = turned(pair)
-                for parity in range(2):
-                    first, second = (pair, back) if parity == 0 else (back, pair)
-                    tile = jnp.concatenate([jnp.where(low, first, zero), jnp.where(low, zero, second)], axis=0)
-                    m = i * KA + kk * YUN + 2 * u + parity
-                    ys[m] = lax.dot_general(
-                        panel_ref[cols_ref[m]], tile, (((1,), (1,)), ((), ())), preferred_element_type=jnp.float32
-                    ).astype(jnp.bfloat16)
+        for k in range(KA):
+            m = i * KA + k
+            col = cols_ref[i, k]
+            ys[m] = lax.dot_general(
+                panel_ref[(col >> 5) * RF + (col & 7)], tiles_ref[m], (((1,), (1,)), ((), ())), preferred_element_type=jnp.float32
+            ).astype(jnp.bfloat16)
 
     @pl.loop(0, SLOTS // WUN)
     def _(step):
@@ -105,7 +109,7 @@
         own_ref[pl.ds(step * 4, 4)] = total(me_ref[0] * CAP + step * 4, 4)
 
 
-def product(cols, route, me, a_tiles, p_tiles, panel):
+def product(cols, route, me, tiles, weights, panel, blanks):
     smem = pl.BlockSpec(memory_space=pltpu.SMEM)
     vmem = pl.BlockSpec(memory_space=pltpu.VMEM)
     return pl.pallas_call(
@@ -113,19 +117,15 @@
         out_shape=(
             jax.ShapeDtypeStruct((POS, LOW, 128), jnp.bfloat16),
             jax.ShapeDtypeStruct((CAP, LOW, 128), jnp.float32),
+            *[BLANK] * NACC,
         ),
-        in_specs=[smem, smem, smem, pl.BlockSpec(memory_space=pltpu.HBM), vmem, vmem],
-        out_specs=(vmem, vmem),
-        scratch_shapes=[
-            pltpu.VMEM((RF, 128, 512), jnp.bfloat16),
-            pltpu.VMEM((SLOTS, ROWS, 128), jnp.bfloat16),
-            pltpu.VMEM((RF, TILE, KA * TILE), jnp.bfloat16),
-            pltpu.SemaphoreType.DMA((1,)),
-        ]
-        + [pltpu.VMEM((POS * LOW, 128), jnp.float32)] * NACC,
+        in_specs=[smem, smem, smem, vmem, vmem, vmem, *[vmem] * NACC],
+        out_specs=(vmem, vmem, *[vmem] * NACC),
+        scratch_shapes=[pltpu.VMEM((SLOTS, ROWS, 128), jnp.bfloat16)],
+        input_output_aliases={6 + n: 2 + n for n in range(NACC)},
         compiler_params=pltpu.CompilerParams(vmem_limit_bytes=16 * 1024 * 1024),
         name="product",
-    )(cols, route, me, a_tiles, p_tiles, panel)
+    )(cols, route, me, tiles, weights, panel, *blanks)[:2]
 
 
 def collect_kernel(slot_ref, rslot_ref, me_ref, own0_ref, own1_ref, recv0_ref, recv1_ref, out_ref, *scratch):
@@ -152,12 +152,14 @@
     low = lane < 64
     even = lax.rem(lane // 32, 2) == 0
 
-    @pl.loop(0, OSLOT // 8)
+    @pl.loop(0, OSLOT // 16)
     def _(g):
-        for quad in range(2):
-            here = pl.ds(g * 8 + quad * 4, 4)
+        quads = range(4)
+        for quad in quads:
+            here = pl.ds(g * 16 + quad * 4, 4)
             block = ((accs[0][here] + accs[1][here]) + (accs[2][here] + accs[3][here])).reshape(128, 128)
             flipped[quad] = block.T
+        for quad in quads:
             parts = [
                 flipped[quad, pl.ds(half * 64 + parity, 32, stride=2), :]
                 for parity in range(2) for half in range(2)
@@ -172,7 +174,8 @@
                 first = jnp.where(even, a, pltpu.roll(b, 32, 1))
                 second = jnp.where(even, pltpu.roll(a, 96, 1), b)
                 for which, value in ((2 * n, first), (2 * n + 1, second)):
-                    out_ref[pl.ds(g * 256 + quad * 4 + which, 32, stride=8), :] = value
+                    row = g * 512 + quad // 2 * 256 + quad % 2 * 4 + which
+                    out_ref[pl.ds(row, 32, stride=8), :] = value
 
 
 def collect(slots, rslots, me, own0, own1, recv0, recv1):
@@ -183,7 +186,7 @@
         out_shape=jax.ShapeDtypeStruct((OSLOT * 32, 128), jnp.float32),
         in_specs=[smem, smem, smem, vmem, vmem, vmem, vmem],
         out_specs=vmem,
-        scratch_shapes=[pltpu.VMEM((OSLOT, 32, 128), jnp.float32)] * 4 + [pltpu.VMEM((2, 128, 128), jnp.float32)],
+        scratch_shapes=[pltpu.VMEM((OSLOT, 32, 128), jnp.float32)] * 4 + [pltpu.VMEM((4, 128, 128), jnp.float32)],
         compiler_params=pltpu.CompilerParams(vmem_limit_bytes=16 * 1024 * 1024),
         name="collect",
     )(slots, rslots, me, own0, own1, recv0, recv1)
@@ -318,8 +321,14 @@
 ORIGINS = [(first, turn, 0, 0) for first, turn in ((0, 0), (0, 1), (1, 0), (1, 1))]
 
 
-def gather_kernel(own_ref, panel_ref, later_ref, send_sem, recv_sems, near_send, near_recv, first_sems, later_sems,
-                  own_sem, transit, later_transit):
+def clear(ref):
+    @pl.loop(0, POS * LOW // 64)
+    def _(step):
+        ref[pl.ds(pl.multiple_of(step * 64, 64), 64), :] = jnp.zeros((64, 128), jnp.float32)
+
+
+def gather_kernel(own_ref, a_hbm, panel_ref, later_ref, tiles_ref, blank0, blank1, blank2, blank3, send_sem, recv_sems, near_send,
+                  near_recv, first_sems, later_sems, own_sem, a_sem, transit, later_transit, a_ref):
     place = Place()
     z = place.high * 4 + place.grp
 
@@ -327,20 +336,16 @@
         level = lax.rem(z + by + 8, 8)
         return place.number(level // 4, place.at, place.core), lax.rem(level, 4)
 
+    fetch = pltpu.make_async_copy(a_hbm, a_ref, a_sem.at[0])
+    fetch.start()
     greet([place.sibling, above(1), above(-1), above(3), above(-3), *place.neighbours.values()])
     start = {(0,) + piece: own_ref.at[0, rows((0,) + piece)] for piece in ORIGINS}
     sems = (send_sem, recv_sems, near_send, near_recv)
+    for number, piece in enumerate(start):
+        remote(start[piece], transit.at[number], send_sem.at[0], first_sems.at[number], above(1 - 2 * piece[2])).start()
     lates = []
 
     def first_leg():
-        for number, piece in enumerate(start):
-            remote(start[piece], transit.at[number], send_sem.at[0], first_sems.at[number],
-                   above(1 - 2 * piece[2])).start()
-        for turn in range(2):
-            part = pl.ds(4 * turn, 4)
-            lates.append(remote(own_ref.at[1, part], later_transit.at[turn], later_sems.at[turn], later_sems.at[2 + turn],
-                                above(1 - 2 * turn)))
-            lates[-1].start()
         remote(own_ref.at[0], panel_ref.at[place.blk], near_send.at[0], near_recv.at[0], place.sibling).start()
         pltpu.make_async_copy(own_ref.at[0], panel_ref.at[place.blk], own_sem.at[0]).start()
         for number, piece in enumerate(start):
@@ -348,6 +353,11 @@
             remote(transit.at[number], transit.at[number], send_sem.at[0], first_sems.at[number], above(up)).wait_recv()
             remote(transit.at[number], panel_ref.at[above(-up)[0], rows(piece)], send_sem.at[0],
                    recv_sems.at[PIECE_ID[(1,) + piece[1:]]], above(3 * up)).start()
+        for turn in range(2):
+            part = pl.ds(4 * turn, 4)
+            lates.append(remote(own_ref.at[1, part], later_transit.at[turn], later_sems.at[turn], later_sems.at[2 + turn],
+                                above(1 - 2 * turn)))
+            lates[-1].start()
 
     def second_leg():
         for turn in range(2):
@@ -356,7 +366,12 @@
                                 later_sems.at[6 + turn], above(3 * (1 - 2 * turn))))
             lates[-1].start()
 
-    spread(place, panel_ref, ORDER_A, start, sems, {0: first_leg, 24: second_leg})
+    between = {0: first_leg, 30: second_leg, 40: fetch.wait}
+    for i in range(RF):
+        between[44 + 8 * i] = functools.partial(build_tiles, a_ref, tiles_ref, i)
+    for n, blank in enumerate((blank0, blank1, blank2, blank3)):
+        between[50 + 16 * n] = functools.partial(clear, blank)
+    spread(place, panel_ref, ORDER_A, start, sems, between)
     pltpu.make_async_copy(own_ref.at[0], panel_ref.at[place.blk], own_sem.at[0]).wait()
     for turn in range(2):
         lates[turn].wait_send()
@@ -377,7 +392,8 @@
     return copies
 
 
-def gather_swap_kernel(own_ref, later_ref, send_ref, slot_ref, panel_ref, recv_ref, rslot_ref, send_sem, recv_sems,
+def gather_swap_kernel(own_ref, later_ref, send_ref, slot_ref, panel_ref, recv_ref, rslot_ref, blank0, blank1, blank2,
+                       blank3, send_sem, recv_sems,
                        near_send, near_recv, own_sems, swap_send, swap_recv, slot_send, slot_recv):
     place = Place()
     greet([place.sibling, *place.neighbours.values(), *partners().values()])
@@ -395,7 +411,10 @@
             copies.append(remote(slot_ref, rslot_ref.at[j - 1], slot_send.at[j - 1], slot_recv.at[j - 1], target))
             copies[-1].start()
 
-    spread(place, panel_ref, ORDER_B, start, (send_sem, recv_sems, near_send, near_recv), {0: rest})
+    between = {0: rest}
+    for n, blank in enumerate((blank0, blank1, blank2, blank3)):
+        between[30 + 20 * n] = functools.partial(clear, blank)
+    spread(place, panel_ref, ORDER_B, start, (send_sem, recv_sems, near_send, near_recv), between)
     for copy in mine:
         copy.wait()
     settle(panel_ref, 30, send_sem.at[0])
@@ -411,10 +430,12 @@
         copy.wait()
 
 
-ORDER_A = arrival_order(slot=0.73, far_slot=1.5, far_latency=5.0)
+ORDER_A = arrival_order(slot=0.73, latency=3.0, far_slot=1.5, far_latency=5.0)
 ORDER_B = arrival_order(slot=0.73, far_slot=0.0, far_latency=0.0)
 ANYWHERE = pl.BlockSpec(memory_space=pl.ANY)
 PANEL = jax.ShapeDtypeStruct((NBLK, RF, ROWS, 128), jnp.bfloat16)
+BLANK = jax.ShapeDtypeStruct((POS * LOW, 128), jnp.float32)
+GATHER_VMEM = 12 << 20
 RECV = jax.ShapeDtypeStruct((3, CAP, LOW, 128), jnp.bfloat16)
 ONE = pltpu.SemaphoreType.DMA((1,))
 TWO = pltpu.SemaphoreType.DMA((2,))
@@ -422,31 +443,39 @@
 MANY = pltpu.SemaphoreType.DMA((len(PIECES),))
 
 
-def gather(own):
+def gather(own, a_tiles):
+    vmem = pl.BlockSpec(memory_space=pltpu.VMEM)
     return pl.pallas_call(
         gather_kernel,
-        out_shape=(PANEL, jax.ShapeDtypeStruct((RF, ROWS, 128), jnp.bfloat16)),
-        in_specs=[ANYWHERE],
-        out_specs=(ANYWHERE, ANYWHERE),
+        out_shape=(
+            PANEL,
+            jax.ShapeDtypeStruct((RF, ROWS, 128), jnp.bfloat16),
+            jax.ShapeDtypeStruct((SLOTS, 128, 128), jnp.bfloat16),
+            *[BLANK] * NACC,
+        ),
+        in_specs=[ANYWHERE, pl.BlockSpec(memory_space=pltpu.HBM)],
+        out_specs=(ANYWHERE, ANYWHERE, vmem, *[vmem] * NACC),
         scratch_shapes=[
-            ONE, MANY, ONE, ONE, pltpu.SemaphoreType.DMA((4,)), pltpu.SemaphoreType.DMA((8,)), ONE,
+            ONE, MANY, ONE, ONE, pltpu.SemaphoreType.DMA((4,)), pltpu.SemaphoreType.DMA((8,)), ONE, ONE,
             pltpu.VMEM((4, 2, ROWS, 128), jnp.bfloat16),
             pltpu.VMEM((2, 4, ROWS, 128), jnp.bfloat16),
+            pltpu.VMEM((RF, TILE, KA * TILE), jnp.bfloat16),
         ],
-        compiler_params=pltpu.CompilerParams(collective_id=0, has_side_effects=True, vmem_limit_bytes=1 << 20),
+        compiler_params=pltpu.CompilerParams(collective_id=0, has_side_effects=True, vmem_limit_bytes=GATHER_VMEM),
         cost_estimate=pl.CostEstimate(flops=0, transcendentals=0, bytes_accessed=1 << 26),
         name="gather",
-    )(own)
+    )(own, a_tiles)
 
 
 def gather_swap(own, later, send, slots):
+    vmem = pl.BlockSpec(memory_space=pltpu.VMEM)
     return pl.pallas_call(
         gather_swap_kernel,
-        out_shape=(PANEL, RECV, jax.ShapeDtypeStruct((3, 2, 128), jnp.int32)),
+        out_shape=(PANEL, RECV, jax.ShapeDtypeStruct((3, 2, 128), jnp.int32), *[BLANK] * NACC),
         in_specs=[ANYWHERE] * 4,
-        out_specs=(ANYWHERE, ANYWHERE, ANYWHERE),
+        out_specs=(ANYWHERE, ANYWHERE, ANYWHERE, *[vmem] * NACC),
         scratch_shapes=[ONE, MANY, ONE, ONE, TWO, THREE, THREE, THREE, THREE],
-        compiler_params=pltpu.CompilerParams(collective_id=1, has_side_effects=True, vmem_limit_bytes=1 << 20),
+        compiler_params=pltpu.CompilerParams(collective_id=1, has_side_effects=True, vmem_limit_bytes=12 << 20),
         cost_estimate=pl.CostEstimate(flops=0, transcendentals=0, bytes_accessed=1 << 26),
         name="gather_swap",
     )(own, later, send, slots)
@@ -464,7 +493,10 @@
     )(send)
 
 
-def arrange_kernel(p_ref, out_ref):
+def arrange_kernel(p_ref, route_ref, out_ref, line_ref, weights_ref):
+    build_weights(p_ref, weights_ref)
+    for half in range(2):
+        line_ref[pl.ds(half, RF, stride=2), :] = route_ref[:, half * 128:(half + 1) * 128] * LOW
     group = lax.broadcasted_iota(jnp.int32, (TILE, 128), 1) // 32
 
     def merged(parts):
@@ -485,29 +517,31 @@
                 out_ref[part, i, q * LOW:(q + 1) * LOW, :] = block[q * 32 + part * LOW:q * 32 + (part + 1) * LOW]
 
 
-def arranged(p_tiles):
+def arranged(p_tiles, route_list):
     vmem = pl.BlockSpec(memory_space=pltpu.VMEM)
     return pl.pallas_call(
         arrange_kernel,
-        out_shape=jax.ShapeDtypeStruct((2, RF, ROWS, 128), jnp.bfloat16),
-        in_specs=[vmem],
-        out_specs=vmem,
+        out_shape=(
+            jax.ShapeDtypeStruct((2, RF, ROWS, 128), jnp.bfloat16),
+            jax.ShapeDtypeStruct((2 * RF, 128), jnp.int32),
+            jax.ShapeDtypeStruct((RF, 128, 512), jnp.bfloat16),
+        ),
+        in_specs=[vmem, vmem],
+        out_specs=(vmem, vmem, vmem),
         compiler_params=pltpu.CompilerParams(vmem_limit_bytes=4 * 1024 * 1024),
         name="arrange",
-    )(p_tiles)
+    )(p_tiles, route_list)
 
 
 def body(a_tiles, a_cols, p_tiles, route_list, out_slot):
     me = lax.axis_index("grp").astype(jnp.int32).reshape(1)
-    cols = a_cols.reshape(SLOTS)
-    cols = cols // (RF * GRP) * RF + cols % RF
-    route = route_list.reshape(RF * 256) * LOW
     slots = out_slot.reshape(2, 128)
-    arranged_tiles = arranged(p_tiles)
-    panel0, later = gather(arranged_tiles)
-    send0, own0 = product(cols, route, me, a_tiles, p_tiles, panel0.reshape(NBLK * RF, ROWS, 128))
-    panel1, recv0, rslots = gather_swap(arranged_tiles, later, send0, slots)
-    send1, own1 = product(cols, route, me, a_tiles, p_tiles, panel1.reshape(NBLK * RF, ROWS, 128))
+    arranged_tiles, route, weights = arranged(p_tiles, route_list)
+    route = route.reshape(RF * 256)
+    panel0, later, tiles, *blank0 = gather(arranged_tiles, a_tiles)
+    send0, own0 = product(a_cols, route, me, tiles, weights, panel0.reshape(NBLK * RF, ROWS, 128), blank0)
+    panel1, recv0, rslots, *blank1 = gather_swap(arranged_tiles, later, send0, slots)
+    send1, own1 = product(a_cols, route, me, tiles, weights, panel1.reshape(NBLK * RF, ROWS, 128), blank1)
     recv1 = exchange(send1)
     out = collect(slots.reshape(POS), rslots.reshape(3 * POS), me, own0, own1, recv0, recv1)
     return out.reshape(16, 32, 8, 128).transpose(0, 2, 1, 3).reshape(OSLOT, TILE * TILE)

time: 139 us -> 127 us (0.914)
  Pallas kernels: 134 us -> 123 us
    pallas_call x2, Pallas kernels: 26.6 us -> 18.6 us  [product(): pl.pallas_call(product_kernel, out_shape=(jax.ShapeDtypeStruct((POS, LOW,...]
    pallas_call x1, Pallas kernels: 42.4 us -> 40.8 us  [gather(): pl.pallas_call(gather_kernel, out_shape=(PANEL, jax.ShapeDtypeStruct((RF,...]
    unnamed x11 -> x10, local copies, waits for them, and re-layouts: 3.13 us -> 3.55 us
where the time goes in v3:
time: 127 us
  Pallas kernels  123 us (97%)
  local copies, waits for them, and re-layouts  3.56 us (3%)
    pallas_call x1, Pallas kernels, gather(): pl.pallas_call(gather_kernel, out_shape=(PANEL, jax.ShapeDtypeStruct((RF,...  40.8 us
    pallas_call x1, Pallas kernels, gather_swap(): pl.pallas_call(gather_swap_kernel, out_shape=(PANEL, RECV, jax.ShapeDtype...  30.2 us
    pallas_call x1, Pallas kernels, exchange(): pl.pallas_call(swap_kernel, out_shape=RECV, in_specs=[ANYWHERE], out_spec...  25.7 us
    pallas_call x2, Pallas kernels, product(): pl.pallas_call(product_kernel, out_shape=(jax.ShapeDtypeStruct((POS, LOW,...  18.6 us
    pallas_call x1, Pallas kernels, collect(): pl.pallas_call(collect_kernel, out_shape=jax.ShapeDtypeStruct((OSLOT * 32...  6.19 us
    unnamed x10, local copies, waits for them, and re-layouts  3.55 us

profile of v3, /device:TPU:1, one launch (start us, length us, event | category | flops | bytes accessed | tf_op | source)
XLA Modules:
  0.0 127.0 jit_solution(5677323831547556652)
XLA Ops:
  0.0 0.0 copy-start.1
  0.0 0.9 copy-done.1
  1.0 0.0 copy-start.3
  1.0 0.7 copy-done.3
  1.6 2.1 %arrange.1 = (bf16[2,8,64,128]{3,2,1,0:T(8,128)(2,1)S(1)}, s32[16,128]{1,0:T(8,128)S(1)}, bf16[8,128,512]{2,1,0:T(8,128)(2,1)S(1)}) custom-call(bf16[8,64,256]{2,1,0:T(8,128)(2,1)S(1)} %copy-done.1, s32[8,256]{1,0:T(8,128)S(1)} %copy-done.3), custom_call_target="tpu_custom_call" | custom-call | tf_op jit(solution)/shard_map/arrange/pallas_call | solution.py:522
  3.7 0.0 copy-start
  3.7 1.2 copy-done
  5.0 40.8 %gather.1 = (bf16[64,8,64,128]{3,2,1,0:T(8,128)(2,1)S(1)}, bf16[8,64,128]{2,1,0:T(8,128)(2,1)S(1)}, bf16[128,128,128]{2,1,0:T(8,128)(2,1)S(1)}, f32[4096,128]{1,...) custom-call(bf16[2,8,64,128]{3,2,1,0:T(8,128)(2,1)S(1)} %get-tuple-element.26.own_ref, ...), custom_call_target="tpu_custom_call" | custom-call | bytes 67108864 | tf_op jit(solution)/shard_map/gather/pallas_call | solution.py:448
  45.7 0.0 copy-start.2
  45.7 0.7 copy-done.2
  46.4 0.0 copy-start.4
  46.4 9.3 %product.2 = (bf16[256,16,128]{2,1,0:T(8,128)(2,1)S(1)}, f32[64,16,128]{2,1,0:T(8,128)S(1)}, f32[4096,128]{1,0:T(8,128)S(1)}, f32[4096,128]{1,0:T(8,128)S(1)}, f...) custom-call(s32[8,16]{1,0:T(8,128)S(1)} %copy-done.2, ...), custom_call_target="tpu_custom_call", output_to_operand_aliasing={{2}: (6, {}), {3}: (7, {}), {4}: (8, {}), {5}: (9, {})} | custom-call | tf_op jit(solution)/shard_map/product/pallas_call | solution.py:115
  55.7 0.0 copy-done.4
  55.7 30.2 %gather_swap.1 = (bf16[64,8,64,128]{3,2,1,0:T(8,128)(2,1)S(1)}, bf16[3,64,16,128]{3,2,1,0:T(8,128)(2,1)S(1)}, s32[3,2,128]{2,1,0:T(2,128)S(1)}, f32[4096,128]{1,...) custom-call(bf16[2,8,64,128]{3,2,1,0:T(8,128)(2,1)S(1)} %get-tuple-element.26.own_ref, ...), custom_call_target="tpu_custom_call" | custom-call | bytes 67108864 | tf_op jit(solution)/shard_map/gather_swap/pallas_call | solution.py:472
  85.9 9.2 %product.3 = (bf16[256,16,128]{2,1,0:T(8,128)(2,1)S(1)}, f32[64,16,128]{2,1,0:T(8,128)S(1)}, f32[4096,128]{1,0:T(8,128)S(1)}, f32[4096,128]{1,0:T(8,128)S(1)}, f...) custom-call(s32[8,16]{1,0:T(8,128)S(1)} %copy-done.2, ...), custom_call_target="tpu_custom_call", output_to_operand_aliasing={{2}: (6, {}), {3}: (7, {}), {4}: (8, {}), {5}: (9, {})} | custom-call | tf_op jit(solution)/shard_map/product/pallas_call | solution.py:115
  95.2 25.7 %exchange.1.recv1_ref = bf16[3,64,16,128]{3,2,1,0:T(8,128)(2,1)S(1)} custom-call(bf16[256,16,128]{2,1,0:T(8,128)(2,1)S(1)} %get-tuple-element.46.send_ref), custom_call_target="tpu_custom_call" | custom-call | tf_op jit(solution)/shard_map/exchange/pallas_call | solution.py:485
  120.8 6.2 %collect.1 = f32[4096,128]{1,0:T(8,128)} custom-call(s32[256]{0:T(256)S(1)} %bitcast.18, s32[768]{0:T(1024)S(1)} %reshape.28.rslot_ref, s32[1]{0:T(128)} %bitcast.2.me_ref, f32[64,16,128]{2,1,0:T(8,128)S(1)} %get-tuple-element.38.own0_ref, f32[64,16,128]{2,1,0:T(8,128)S(1)} %get-tuple-element.44.own1_ref, ...), custom_call_target="tpu_custom_call" | custom-call | tf_op jit(solution)/shard_map/collect/pallas_call | solution.py:184
  (1 shorter events, 0.0 us)
Async XLA Ops:
  0.0 0.9 copy-start.1
  1.0 0.7 copy-start.3
  3.7 1.2 copy-start
  45.7 0.7 copy-start.2
  46.4 9.3 %copy-start.4 = (s32[1,256]{1,0:T(1,128)S(1)}, s32[1,256]{1,0:T(1,128)}, u32[]{:S(2)}) copy-start(s32[1,256]{1,0:T(1,128)} %param.9) | copy-start | bytes 3076

commit v4 on v3

--- a/solution.py
+++ b/solution.py
@@ -63,7 +63,7 @@
             tiles_ref[m, TILE:128, :] = jnp.where(low, zero, second)
 
 
-def product_kernel(cols_ref, route_ref, me_ref, tiles_ref, weights, panel_ref, blank0, blank1, blank2, blank3, send_ref,
+def product_kernel(lines_ref, me_ref, tiles_ref, weights, panel_ref, blank0, blank1, blank2, blank3, send_ref,
                    own_ref, acc0, acc1, acc2, acc3, ys):
     accs = (acc0, acc1, acc2, acc3)
 
@@ -71,7 +71,7 @@
     def _(i):
         for k in range(KA):
             m = i * KA + k
-            col = cols_ref[i, k]
+            col = lines_ref[2 * RF * 128 + i * 128 + k]
             ys[m] = lax.dot_general(
                 panel_ref[(col >> 5) * RF + (col & 7)], tiles_ref[m], (((1,), (1,)), ((), ())), preferred_element_type=jnp.float32
             ).astype(jnp.bfloat16)
@@ -89,7 +89,7 @@
         for u in range(WUN):
             for q in range(KP):
                 for s in range(KP):
-                    r = route_ref[base + (s * KA + u) * KP + q]
+                    r = lines_ref[base + (s * KA + u) * KP + q]
                     acc = accs[s % NACC]
                     row, lane = u * ROWS + q * LOW, s % 2 * 128
                     here = pl.ds(pl.multiple_of(r, LOW), LOW)
@@ -109,7 +109,7 @@
         own_ref[pl.ds(step * 4, 4)] = total(me_ref[0] * CAP + step * 4, 4)
 
 
-def product(cols, route, me, tiles, weights, panel, blanks):
+def product(lines, me, tiles, weights, panel, blanks):
     smem = pl.BlockSpec(memory_space=pltpu.SMEM)
     vmem = pl.BlockSpec(memory_space=pltpu.VMEM)
     return pl.pallas_call(
@@ -119,23 +119,19 @@
             jax.ShapeDtypeStruct((CAP, LOW, 128), jnp.float32),
             *[BLANK] * NACC,
         ),
-        in_specs=[smem, smem, smem, vmem, vmem, vmem, *[vmem] * NACC],
+        in_specs=[smem, smem, vmem, vmem, vmem, *[vmem] * NACC],
         out_specs=(vmem, vmem, *[vmem] * NACC),
         scratch_shapes=[pltpu.VMEM((SLOTS, ROWS, 128), jnp.bfloat16)],
-        input_output_aliases={6 + n: 2 + n for n in range(NACC)},
+        input_output_aliases={5 + n: 2 + n for n in range(NACC)},
         compiler_params=pltpu.CompilerParams(vmem_limit_bytes=16 * 1024 * 1024),
         name="product",
-    )(cols, route, me, tiles, weights, panel, *blanks)[:2]
-
-
-def collect_kernel(slot_ref, rslot_ref, me_ref, own0_ref, own1_ref, recv0_ref, recv1_ref, out_ref, *scratch):
-    accs, flipped = scratch[:4], scratch[4]
+    )(lines, me, tiles, weights, panel, *blanks)[:2]
+
+
+def collect_kernel(slot_ref, rslot_ref, me_ref, own0_ref, own1_ref, recv0_ref, recv1_ref, blank0, blank1, blank2, blank3,
+                   out_ref, acc0, acc1, acc2, acc3, flipped):
+    accs = (acc0, acc1, acc2, acc3)
     me = me_ref[0]
-
-    @pl.loop(0, OSLOT // 2)
-    def _(b):
-        for acc in accs:
-            acc[pl.ds(b * 2, 2)] = jnp.zeros((2, 32, 128), jnp.float32)
 
     @pl.loop(0, CAP // 2)
     def _(step):
@@ -145,8 +141,10 @@
                 b = slot_ref[me * CAP + p] if j == 3 else rslot_ref[j * POS + me * CAP + p]
                 low = own0_ref[p] if j == 3 else recv0_ref[j, p].astype(jnp.float32)
                 high = own1_ref[p] if j == 3 else recv1_ref[j, p].astype(jnp.float32)
-                accs[j][b, 0:LOW] = accs[j][b, 0:LOW] + low
-                accs[j][b, LOW:] = accs[j][b, LOW:] + high
+                here = pl.ds(pl.multiple_of(b * 32, 32), LOW)
+                there = pl.ds(pl.multiple_of(b * 32 + LOW, LOW), LOW)
+                accs[j][here, :] = accs[j][here, :] + low
+                accs[j][there, :] = accs[j][there, :] + high
 
     lane = lax.broadcasted_iota(jnp.int32, (32, 128), 1)
     low = lane < 64
@@ -156,8 +154,8 @@
     def _(g):
         quads = range(4)
         for quad in quads:
-            here = pl.ds(g * 16 + quad * 4, 4)
-            block = ((accs[0][here] + accs[1][here]) + (accs[2][here] + accs[3][here])).reshape(128, 128)
+            here = pl.ds(pl.multiple_of(g * 512 + quad * 128, 128), 128)
+            block = (accs[0][here, :] + accs[1][here, :]) + (accs[2][here, :] + accs[3][here, :])
             flipped[quad] = block.T
         for quad in quads:
             parts = [
@@ -178,18 +176,19 @@
                     out_ref[pl.ds(row, 32, stride=8), :] = value
 
 
-def collect(slots, rslots, me, own0, own1, recv0, recv1):
+def collect(slots, rslots, me, own0, own1, recv0, recv1, blanks):
     smem = pl.BlockSpec(memory_space=pltpu.SMEM)
     vmem = pl.BlockSpec(memory_space=pltpu.VMEM)
     return pl.pallas_call(
         collect_kernel,
-        out_shape=jax.ShapeDtypeStruct((OSLOT * 32, 128), jnp.float32),
-        in_specs=[smem, smem, smem, vmem, vmem, vmem, vmem],
-        out_specs=vmem,
-        scratch_shapes=[pltpu.VMEM((OSLOT, 32, 128), jnp.float32)] * 4 + [pltpu.VMEM((4, 128, 128), jnp.float32)],
+        out_shape=(jax.ShapeDtypeStruct((OSLOT * 32, 128), jnp.float32), *[BLANK] * 4),
+        in_specs=[smem, smem, smem, vmem, vmem, vmem, vmem, *[vmem] * 4],
+        out_specs=(vmem, *[vmem] * 4),
+        scratch_shapes=[pltpu.VMEM((4, 128, 128), jnp.float32)],
+        input_output_aliases={7 + n: 1 + n for n in range(4)},
         compiler_params=pltpu.CompilerParams(vmem_limit_bytes=16 * 1024 * 1024),
         name="collect",
-    )(slots, rslots, me, own0, own1, recv0, recv1)
+    )(slots, rslots, me, own0, own1, recv0, recv1, *blanks)[0]
 
 
 NBLK = 64
@@ -327,8 +326,8 @@
         ref[pl.ds(pl.multiple_of(step * 64, 64), 64), :] = jnp.zeros((64, 128), jnp.float32)
 
 
-def gather_kernel(own_ref, a_hbm, panel_ref, later_ref, tiles_ref, blank0, blank1, blank2, blank3, send_sem, recv_sems, near_send,
-                  near_recv, first_sems, later_sems, own_sem, a_sem, transit, later_transit, a_ref):
+def gather_kernel(own_ref, a_hbm, p_hbm, panel_ref, later_ref, tiles_ref, weights_ref, blank0, blank1, blank2, blank3, send_sem, recv_sems, near_send,
+                  near_recv, first_sems, later_sems, own_sem, a_sem, transit, later_transit, a_ref, p_ref):
     place = Place()
     z = place.high * 4 + place.grp
 
@@ -338,6 +337,8 @@
 
     fetch = pltpu.make_async_copy(a_hbm, a_ref, a_sem.at[0])
     fetch.start()
+    fetch_p = pltpu.make_async_copy(p_hbm, p_ref, a_sem.at[1])
+    fetch_p.start()
     greet([place.sibling, above(1), above(-1), above(3), above(-3), *place.neighbours.values()])
     start = {(0,) + piece: own_ref.at[0, rows((0,) + piece)] for piece in ORIGINS}
     sems = (send_sem, recv_sems, near_send, near_recv)
@@ -367,6 +368,12 @@
             lates[-1].start()
 
     between = {0: first_leg, 30: second_leg, 40: fetch.wait}
+
+    def weights():
+        fetch_p.wait()
+        build_weights(p_ref, weights_ref)
+
+    between[36] = weights
     for i in range(RF):
         between[44 + 8 * i] = functools.partial(build_tiles, a_ref, tiles_ref, i)
     for n, blank in enumerate((blank0, blank1, blank2, blank3)):
@@ -424,9 +431,12 @@
         copy.wait()
 
 
-def swap_kernel(send_ref, recv_ref, swap_send, swap_recv):
+def swap_kernel(send_ref, recv_ref, blank0, blank1, blank2, blank3, swap_send, swap_recv):
     greet(list(partners().values()))
-    for copy in swap(send_ref, recv_ref, (swap_send, swap_recv)):
+    copies = swap(send_ref, recv_ref, (swap_send, swap_recv))
+    for blank in (blank0, blank1, blank2, blank3):
+        clear(blank)
+    for copy in copies:
         copy.wait()
 
 
@@ -435,7 +445,7 @@
 ANYWHERE = pl.BlockSpec(memory_space=pl.ANY)
 PANEL = jax.ShapeDtypeStruct((NBLK, RF, ROWS, 128), jnp.bfloat16)
 BLANK = jax.ShapeDtypeStruct((POS * LOW, 128), jnp.float32)
-GATHER_VMEM = 12 << 20
+GATHER_VMEM = 20 << 20
 RECV = jax.ShapeDtypeStruct((3, CAP, LOW, 128), jnp.bfloat16)
 ONE = pltpu.SemaphoreType.DMA((1,))
 TWO = pltpu.SemaphoreType.DMA((2,))
@@ -443,7 +453,7 @@
 MANY = pltpu.SemaphoreType.DMA((len(PIECES),))
 
 
-def gather(own, a_tiles):
+def gather(own, a_tiles, p_tiles):
     vmem = pl.BlockSpec(memory_space=pltpu.VMEM)
     return pl.pallas_call(
         gather_kernel,
@@ -451,20 +461,22 @@
             PANEL,
             jax.ShapeDtypeStruct((RF, ROWS, 128), jnp.bfloat16),
             jax.ShapeDtypeStruct((SLOTS, 128, 128), jnp.bfloat16),
+            jax.ShapeDtypeStruct((RF, 128, 512), jnp.bfloat16),
             *[BLANK] * NACC,
         ),
-        in_specs=[ANYWHERE, pl.BlockSpec(memory_space=pltpu.HBM)],
-        out_specs=(ANYWHERE, ANYWHERE, vmem, *[vmem] * NACC),
+        in_specs=[ANYWHERE] + [pl.BlockSpec(memory_space=pltpu.HBM)] * 2,
+        out_specs=(ANYWHERE, ANYWHERE, vmem, vmem, *[vmem] * NACC),
         scratch_shapes=[
-            ONE, MANY, ONE, ONE, pltpu.SemaphoreType.DMA((4,)), pltpu.SemaphoreType.DMA((8,)), ONE, ONE,
+            ONE, MANY, ONE, ONE, pltpu.SemaphoreType.DMA((4,)), pltpu.SemaphoreType.DMA((8,)), ONE, TWO,
             pltpu.VMEM((4, 2, ROWS, 128), jnp.bfloat16),
             pltpu.VMEM((2, 4, ROWS, 128), jnp.bfloat16),
             pltpu.VMEM((RF, TILE, KA * TILE), jnp.bfloat16),
+            pltpu.VMEM((RF, TILE, KP * TILE), jnp.bfloat16),
         ],
         compiler_params=pltpu.CompilerParams(collective_id=0, has_side_effects=True, vmem_limit_bytes=GATHER_VMEM),
         cost_estimate=pl.CostEstimate(flops=0, transcendentals=0, bytes_accessed=1 << 26),
         name="gather",
-    )(own, a_tiles)
+    )(own, a_tiles, p_tiles)
 
 
 def gather_swap(own, later, send, slots):
@@ -475,7 +487,7 @@
         in_specs=[ANYWHERE] * 4,
         out_specs=(ANYWHERE, ANYWHERE, ANYWHERE, *[vmem] * NACC),
         scratch_shapes=[ONE, MANY, ONE, ONE, TWO, THREE, THREE, THREE, THREE],
-        compiler_params=pltpu.CompilerParams(collective_id=1, has_side_effects=True, vmem_limit_bytes=12 << 20),
+        compiler_params=pltpu.CompilerParams(collective_id=1, has_side_effects=True, vmem_limit_bytes=GATHER_VMEM),
         cost_estimate=pl.CostEstimate(flops=0, transcendentals=0, bytes_accessed=1 << 26),
         name="gather_swap",
     )(own, later, send, slots)
@@ -484,17 +496,26 @@
 def exchange(send):
     return pl.pallas_call(
         swap_kernel,
-        out_shape=RECV,
+        out_shape=(RECV, *[BLANK] * 4),
         in_specs=[ANYWHERE],
-        out_specs=ANYWHERE,
+        out_specs=(ANYWHERE, *[pl.BlockSpec(memory_space=pltpu.VMEM)] * 4),
         scratch_shapes=[THREE, THREE],
-        compiler_params=pltpu.CompilerParams(collective_id=2, has_side_effects=True, vmem_limit_bytes=1 << 20),
+        compiler_params=pltpu.CompilerParams(collective_id=2, has_side_effects=True, vmem_limit_bytes=12 << 20),
         name="exchange",
     )(send)
 
 
-def arrange_kernel(p_ref, route_ref, out_ref, line_ref, weights_ref):
-    build_weights(p_ref, weights_ref)
+def arrange_kernel(p_hbm, route_hbm, cols_hbm, out_ref, line_ref, p_ref, route_ref, cols_ref, sems):
+    copies = [
+        pltpu.make_async_copy(source, target, sems.at[number])
+        for number, (source, target) in enumerate(((p_hbm, p_ref), (route_hbm, route_ref), (cols_hbm, cols_ref)))
+    ]
+    for copy in copies:
+        copy.start()
+    for copy in copies:
+        copy.wait()
+    line_ref[2 * RF:3 * RF, :] = jnp.zeros((RF, 128), jnp.int32)
+    line_ref[2 * RF:3 * RF, 0:KA] = cols_ref[...]
     for half in range(2):
         line_ref[pl.ds(half, RF, stride=2), :] = route_ref[:, half * 128:(half + 1) * 128] * LOW
     group = lax.broadcasted_iota(jnp.int32, (TILE, 128), 1) // 32
@@ -517,33 +538,41 @@
                 out_ref[part, i, q * LOW:(q + 1) * LOW, :] = block[q * 32 + part * LOW:q * 32 + (part + 1) * LOW]
 
 
-def arranged(p_tiles, route_list):
+def arranged(*arrays):
     vmem = pl.BlockSpec(memory_space=pltpu.VMEM)
     return pl.pallas_call(
         arrange_kernel,
         out_shape=(
             jax.ShapeDtypeStruct((2, RF, ROWS, 128), jnp.bfloat16),
-            jax.ShapeDtypeStruct((2 * RF, 128), jnp.int32),
-            jax.ShapeDtypeStruct((RF, 128, 512), jnp.bfloat16),
+            jax.ShapeDtypeStruct((3 * RF, 128), jnp.int32),
         ),
-        in_specs=[vmem, vmem],
-        out_specs=(vmem, vmem, vmem),
+        in_specs=[pl.BlockSpec(memory_space=pltpu.HBM)] * 3,
+        out_specs=(vmem, vmem),
+        scratch_shapes=[
+            pltpu.VMEM((RF, TILE, KP * TILE), jnp.bfloat16),
+            pltpu.VMEM((RF, 256), jnp.int32),
+            pltpu.VMEM((RF, KA), jnp.int32),
+            THREE,
+        ],
         compiler_params=pltpu.CompilerParams(vmem_limit_bytes=4 * 1024 * 1024),
         name="arrange",
-    )(p_tiles, route_list)
+    )(*[pltpu.with_memory_space_constraint(array, pltpu.HBM) for array in arrays])
 
 
 def body(a_tiles, a_cols, p_tiles, route_list, out_slot):
     me = lax.axis_index("grp").astype(jnp.int32).reshape(1)
     slots = out_slot.reshape(2, 128)
-    arranged_tiles, route, weights = arranged(p_tiles, route_list)
-    route = route.reshape(RF * 256)
-    panel0, later, tiles, *blank0 = gather(arranged_tiles, a_tiles)
-    send0, own0 = product(a_cols, route, me, tiles, weights, panel0.reshape(NBLK * RF, ROWS, 128), blank0)
-    panel1, recv0, rslots, *blank1 = gather_swap(arranged_tiles, later, send0, slots)
-    send1, own1 = product(a_cols, route, me, tiles, weights, panel1.reshape(NBLK * RF, ROWS, 128), blank1)
-    recv1 = exchange(send1)
-    out = collect(slots.reshape(POS), rslots.reshape(3 * POS), me, own0, own1, recv0, recv1)
+    arranged_tiles, lines = arranged(p_tiles, route_list, a_cols)
+    lines = lines.reshape(3 * RF * 128)
+    a_tiles = pltpu.with_memory_space_constraint(a_tiles, pltpu.HBM)
+    p_tiles = pltpu.with_memory_space_constraint(p_tiles, pltpu.HBM)
+    panel0, later, tiles, weights, *blank0 = gather(arranged_tiles, a_tiles, p_tiles)
+    send0, own0 = product(lines, me, tiles, weights, panel0.reshape(NBLK * RF, ROWS, 128), blank0)
+    panel1, recv0, rslots, *blank1 = gather_swap(
+        arranged_tiles, later, send0, pltpu.with_memory_space_constraint(slots, pltpu.HBM))
+    send1, own1 = product(lines, me, tiles, weights, panel1.reshape(NBLK * RF, ROWS, 128), blank1)
+    recv1, *blank = exchange(send1)
+    out = collect(slots.reshape(POS), rslots.reshape(3 * POS), me, own0, own1, recv0, recv1, blank)
     return out.reshape(16, 32, 8, 128).transpose(0, 2, 1, 3).reshape(OSLOT, TILE * TILE)
 
 

time: 127 us -> 123 us (0.969)
  local copies, waits for them, and re-layouts: 3.56 us -> 0.02 us
    unnamed x10 -> x2, local copies, waits for them, and re-layouts: 3.55 us -> 0.01 us
where the time goes in v4:
time: 123 us
  Pallas kernels  123 us (100%)
    pallas_call x1, Pallas kernels, gather(): pl.pallas_call(gather_kernel, out_shape=(PANEL, jax.ShapeDtypeStruct((RF,...  40.9 us
    pallas_call x1, Pallas kernels, gather_swap(): pl.pallas_call(gather_swap_kernel, out_shape=(PANEL, RECV, jax.ShapeDtype...  30.1 us
    pallas_call x1, Pallas kernels, exchange(): pl.pallas_call(swap_kernel, out_shape=(RECV, *[BLANK] * 4), in_specs=[ANY...  25.6 us
    pallas_call x2, Pallas kernels, product(): pl.pallas_call(product_kernel, out_shape=(jax.ShapeDtypeStruct((POS, LOW,...  18.5 us
    pallas_call x1, Pallas kernels, collect(): pl.pallas_call(collect_kernel, out_shape=(jax.ShapeDtypeStruct((OSLOT * 3...  5.68 us

profile of v4, /device:TPU:1, one launch (start us, length us, event | category | flops | bytes accessed | tf_op | source)
XLA Modules:
  0.0 123.4 jit_solution(6936712304037057123)
XLA Ops:
  0.0 2.4 %arrange.1 = (bf16[2,8,64,128]{3,2,1,0:T(8,128)(2,1)S(1)}, s32[24,128]{1,0:T(8,128)S(1)}) custom-call(bf16[8,64,256]{2,1,0:T(8,128)(2,1)} %p_hbm.3, s32[8,256]{1,0:T(8,128)} %route_hbm.1, s32[8,16]{1,0:T(8,128)} %cols_hbm.1), custom_call_target="tpu_custom_call" | custom-call | tf_op jit(solution)/shard_map/arrange/pallas_call | solution.py:543
  2.4 40.9 %gather.1 = (bf16[64,8,64,128]{3,2,1,0:T(8,128)(2,1)S(1)}, bf16[8,64,128]{2,1,0:T(8,128)(2,1)S(1)}, bf16[128,128,128]{2,1,0:T(8,128)(2,1)S(1)}, bf16[8,128,512]{...) custom-call(bf16[2,8,64,128]{3,2,1,0:T(8,128)(2,1)S(1)} %get-tuple-e, ...), custom_call_target="tpu_custom_call" | custom-call | bytes 67108864 | tf_op jit(solution)/shard_map/gather/pallas_call | solution.py:458
  43.3 9.3 %product.2 = (bf16[256,16,128]{2,1,0:T(8,128)(2,1)S(1)}, f32[64,16,128]{2,1,0:T(8,128)S(1)}, f32[4096,128]{1,0:T(8,128)S(1)}, f32[4096,128]{1,0:T(8,128)S(1)}, f...) custom-call(s32[3072]{0:T(1024)S(1)} %bitcast.15, ...), custom_call_target="tpu_custom_call", output_to_operand_aliasing={{2}: (5, {}), {3}: (6, {}), {4}: (7, {}), {5}: (8, {})} | custom-call | tf_op jit(solution)/shard_map/product/pallas_call | solution.py:115
  52.5 30.1 %gather_swap.1 = (bf16[64,8,64,128]{3,2,1,0:T(8,128)(2,1)S(1)}, bf16[3,64,16,128]{3,2,1,0:T(8,128)(2,1)S(1)}, s32[3,2,128]{2,1,0:T(2,128)S(1)}, f32[4096,128]{1,...) custom-call(bf16[2,8,64,128]{3,2,1,0:T(8,128)(2,1)S(1)} %get-tuple-element.32.own_ref, ...), custom_call_target="tpu_custom_call" | custom-call | bytes 67108864 | tf_op jit(solution)/shard_map/gather_swap/pallas_call | solution.py:484
  82.7 0.0 copy-start
  82.7 9.3 %product.3 = (bf16[256,16,128]{2,1,0:T(8,128)(2,1)S(1)}, f32[64,16,128]{2,1,0:T(8,128)S(1)}, f32[4096,128]{1,0:T(8,128)S(1)}, f32[4096,128]{1,0:T(8,128)S(1)}, f...) custom-call(s32[3072]{0:T(1024)S(1)} %bitcast.16, ...), custom_call_target="tpu_custom_call", output_to_operand_aliasing={{2}: (5, {}), {3}: (6, {}), {4}: (7, {}), {5}: (8, {})} | custom-call | tf_op jit(solution)/shard_map/product/pallas_call | solution.py:115
  92.0 25.6 %exchange.1 = (bf16[3,64,16,128]{3,2,1,0:T(8,128)(2,1)S(1)}, f32[4096,128]{1,0:T(8,128)S(1)}, f32[4096,128]{1,0:T(8,128)S(1)}, f32[4096,128]{1,0:T(8,128)S(1)}, f32[4096,128]{1,0:T(8,128)S(1)}) custom-call(bf16[256,16,128]{2,1,0:T(8,128)(2,1)S(1)} %get-tuple-element.52.send_ref), custom_call_target="tpu_custom_call" | custom-call | tf_op jit(solution)/shard_map/exchange/pallas_call | solution.py:497
  117.7 0.0 copy-done
  117.7 5.7 %collect.1 = (f32[4096,128]{1,0:T(8,128)}, f32[4096,128]{1,0:T(8,128)S(1)}, f32[4096,128]{1,0:T(8,128)S(1)}, f32[4096,128]{1,0:T(8,128)S(1)}, f32[4096,128]{1,0:T(8,128)S(1)}) custom-call(s32[256]{0:T(256)S(1)} %bitcast.18, s32[768]{0:T(1024)S(1)} %reshape.28.rslot_ref, ...), custom_call_target="tpu_custom_call", output_to_operand_aliasing={{1}: (7, {}), {2}: (8, {}), {3}: (9, {}), {4}: (10, {})} | custom-call | tf_op jit(solution)/shard_map/collect/pallas_call | solution.py:182
  (1 shorter events, 0.0 us)
Async XLA Ops:
  82.7 35.0 %copy-start = (s32[1,256]{1,0:T(1,128)S(1)}, s32[1,256]{1,0:T(1,128)}, u32[]{:S(2)}) copy-start(s32[1,256]{1,0:T(1,128)} %param.9) | copy-start | bytes 3076

commit v5 on v4

--- a/solution.py
+++ b/solution.py
@@ -129,7 +129,7 @@
 
 
 def collect_kernel(slot_ref, rslot_ref, me_ref, own0_ref, own1_ref, recv0_ref, recv1_ref, blank0, blank1, blank2, blank3,
-                   out_ref, acc0, acc1, acc2, acc3, flipped):
+                   out_hbm, acc0, acc1, acc2, acc3, flipped, out_ref, out_sems):
     accs = (acc0, acc1, acc2, acc3)
     me = me_ref[0]
 
@@ -150,8 +150,16 @@
     low = lane < 64
     even = lax.rem(lane // 32, 2) == 0
 
+    def leave(g):
+        part = pl.ds(pl.multiple_of(g * 512, 512), 512)
+        return pltpu.make_async_copy(out_ref.at[part, :], out_hbm.at[part, :], out_sems.at[g])
+
     @pl.loop(0, OSLOT // 16)
     def _(g):
+        @pl.when(g > 0)
+        def _():
+            leave(g - 1).start()
+
         quads = range(4)
         for quad in quads:
             here = pl.ds(pl.multiple_of(g * 512 + quad * 128, 128), 128)
@@ -175,6 +183,12 @@
                     row = g * 512 + quad // 2 * 256 + quad % 2 * 4 + which
                     out_ref[pl.ds(row, 32, stride=8), :] = value
 
+    for g in range(OSLOT // 16 - 1):
+        leave(g).wait()
+    last = leave(OSLOT // 16 - 1)
+    last.start()
+    last.wait()
+
 
 def collect(slots, rslots, me, own0, own1, recv0, recv1, blanks):
     smem = pl.BlockSpec(memory_space=pltpu.SMEM)
@@ -183,8 +197,12 @@
         collect_kernel,
         out_shape=(jax.ShapeDtypeStruct((OSLOT * 32, 128), jnp.float32), *[BLANK] * 4),
         in_specs=[smem, smem, smem, vmem, vmem, vmem, vmem, *[vmem] * 4],
-        out_specs=(vmem, *[vmem] * 4),
-        scratch_shapes=[pltpu.VMEM((4, 128, 128), jnp.float32)],
+        out_specs=(pl.BlockSpec(memory_space=pltpu.HBM), *[vmem] * 4),
+        scratch_shapes=[
+            pltpu.VMEM((4, 128, 128), jnp.float32),
+            pltpu.VMEM((OSLOT * 32, 128), jnp.float32),
+            pltpu.SemaphoreType.DMA((OSLOT // 16,)),
+        ],
         input_output_aliases={7 + n: 1 + n for n in range(4)},
         compiler_params=pltpu.CompilerParams(vmem_limit_bytes=16 * 1024 * 1024),
         name="collect",
@@ -526,16 +544,18 @@
             value = jnp.where(group == number, parts[number], value)
         return value
 
-    @pl.loop(0, RF)
-    def _(i):
-        left = p_ref[i, :, 0:128].astype(jnp.float32)
-        right = p_ref[i, :, 128:256].astype(jnp.float32)
-        first = merged([left, pltpu.roll(left, 96, 1), pltpu.roll(right, 64, 1), pltpu.roll(right, 32, 1)])
-        second = merged([pltpu.roll(left, 96, 1), pltpu.roll(left, 64, 1), pltpu.roll(right, 32, 1), right])
-        block = jnp.concatenate([first, second], axis=0).T.astype(jnp.bfloat16)
-        for q in range(KP):
-            for part in range(2):
-                out_ref[part, i, q * LOW:(q + 1) * LOW, :] = block[q * 32 + part * LOW:q * 32 + (part + 1) * LOW]
+    @pl.loop(0, RF // 2)
+    def _(step):
+        for e in range(2):
+            i = step * 2 + e
+            left = p_ref[i, :, 0:128].astype(jnp.float32)
+            right = p_ref[i, :, 128:256].astype(jnp.float32)
+            first = merged([left, pltpu.roll(left, 96, 1), pltpu.roll(right, 64, 1), pltpu.roll(right, 32, 1)])
+            second = merged([pltpu.roll(left, 96, 1), pltpu.roll(left, 64, 1), pltpu.roll(right, 32, 1), right])
+            block = jnp.concatenate([first, second], axis=0).T.astype(jnp.bfloat16)
+            for q in range(KP):
+                for part in range(2):
+                    out_ref[part, i, q * LOW:(q + 1) * LOW, :] = block[q * 32 + part * LOW:q * 32 + (part + 1) * LOW]
 
 
 def arranged(*arrays):

time: 123 us -> 123 us (level)
  no operation moved by 1% of the time
where the time goes in v5:
time: 123 us
  Pallas kernels  122 us (99%)
    pallas_call x1, Pallas kernels, gather(): pl.pallas_call(gather_kernel, out_shape=(PANEL, jax.ShapeDtypeStruct((RF,...  40.9 us
    pallas_call x1, Pallas kernels, gather_swap(): pl.pallas_call(gather_swap_kernel, out_shape=(PANEL, RECV, jax.ShapeDtype...  30.1 us
    pallas_call x1, Pallas kernels, exchange(): pl.pallas_call(swap_kernel, out_shape=(RECV, *[BLANK] * 4), in_specs=[ANY...  25.7 us
    pallas_call x2, Pallas kernels, product(): pl.pallas_call(product_kernel, out_shape=(jax.ShapeDtypeStruct((POS, LOW,...  18.6 us
    pallas_call x1, Pallas kernels, collect(): pl.pallas_call(collect_kernel, out_shape=(jax.ShapeDtypeStruct((OSLOT * 3...  5.45 us

profile of v5, /device:TPU:1, one launch (start us, length us, event | category | flops | bytes accessed | tf_op | source)
XLA Modules:
  0.0 122.5 jit_solution(12567306230082332718)
XLA Ops:
  0.0 1.8 %arrange.1 = (bf16[2,8,64,128]{3,2,1,0:T(8,128)(2,1)S(1)}, s32[24,128]{1,0:T(8,128)S(1)}) custom-call(bf16[8,64,256]{2,1,0:T(8,128)(2,1)} %p_hbm.3, s32[8,256]{1,0:T(8,128)} %route_hbm.1, s32[8,16]{1,0:T(8,128)} %cols_hbm.1), custom_call_target="tpu_custom_call" | custom-call | tf_op jit(solution)/shard_map/arrange/pallas_call | solution.py:563
  1.8 40.9 %gather.1 = (bf16[64,8,64,128]{3,2,1,0:T(8,128)(2,1)S(1)}, bf16[8,64,128]{2,1,0:T(8,128)(2,1)S(1)}, bf16[128,128,128]{2,1,0:T(8,128)(2,1)S(1)}, bf16[8,128,512]{...) custom-call(bf16[2,8,64,128]{3,2,1,0:T(8,128)(2,1)S(1)} %get-tuple-e, ...), custom_call_target="tpu_custom_call" | custom-call | bytes 67108864 | tf_op jit(solution)/shard_map/gather/pallas_call | solution.py:476
  42.7 9.3 %product.2 = (bf16[256,16,128]{2,1,0:T(8,128)(2,1)S(1)}, f32[64,16,128]{2,1,0:T(8,128)S(1)}, f32[4096,128]{1,0:T(8,128)S(1)}, f32[4096,128]{1,0:T(8,128)S(1)}, f...) custom-call(s32[3072]{0:T(1024)S(1)} %bitcast.15, ...), custom_call_target="tpu_custom_call", output_to_operand_aliasing={{2}: (5, {}), {3}: (6, {}), {4}: (7, {}), {5}: (8, {})} | custom-call | tf_op jit(solution)/shard_map/product/pallas_call | solution.py:115
  52.0 30.1 %gather_swap.1 = (bf16[64,8,64,128]{3,2,1,0:T(8,128)(2,1)S(1)}, bf16[3,64,16,128]{3,2,1,0:T(8,128)(2,1)S(1)}, s32[3,2,128]{2,1,0:T(2,128)S(1)}, f32[4096,128]{1,...) custom-call(bf16[2,8,64,128]{3,2,1,0:T(8,128)(2,1)S(1)} %get-tuple-element.32.own_ref, ...), custom_call_target="tpu_custom_call" | custom-call | bytes 67108864 | tf_op jit(solution)/shard_map/gather_swap/pallas_call | solution.py:502
  82.1 0.0 copy-start
  82.1 9.3 %product.3 = (bf16[256,16,128]{2,1,0:T(8,128)(2,1)S(1)}, f32[64,16,128]{2,1,0:T(8,128)S(1)}, f32[4096,128]{1,0:T(8,128)S(1)}, f32[4096,128]{1,0:T(8,128)S(1)}, f...) custom-call(s32[3072]{0:T(1024)S(1)} %bitcast.16, ...), custom_call_target="tpu_custom_call", output_to_operand_aliasing={{2}: (5, {}), {3}: (6, {}), {4}: (7, {}), {5}: (8, {})} | custom-call | tf_op jit(solution)/shard_map/product/pallas_call | solution.py:115
  91.4 25.7 %exchange.1 = (bf16[3,64,16,128]{3,2,1,0:T(8,128)(2,1)S(1)}, f32[4096,128]{1,0:T(8,128)S(1)}, f32[4096,128]{1,0:T(8,128)S(1)}, f32[4096,128]{1,0:T(8,128)S(1)}, f32[4096,128]{1,0:T(8,128)S(1)}) custom-call(bf16[256,16,128]{2,1,0:T(8,128)(2,1)S(1)} %get-tuple-element.52.send_ref), custom_call_target="tpu_custom_call" | custom-call | tf_op jit(solution)/shard_map/exchange/pallas_call | solution.py:515
  117.1 0.0 copy-done
  117.1 5.4 %collect.1 = (f32[4096,128]{1,0:T(8,128)}, f32[4096,128]{1,0:T(8,128)S(1)}, f32[4096,128]{1,0:T(8,128)S(1)}, f32[4096,128]{1,0:T(8,128)S(1)}, f32[4096,128]{1,0:T(8,128)S(1)}) custom-call(s32[256]{0:T(256)S(1)} %bitcast.18, s32[768]{0:T(1024)S(1)} %reshape.28.rslot_ref, ...), custom_call_target="tpu_custom_call", output_to_operand_aliasing={{1}: (7, {}), {2}: (8, {}), {3}: (9, {}), {4}: (10, {})} | custom-call | tf_op jit(solution)/shard_map/collect/pallas_call | solution.py:196
  (1 shorter events, 0.0 us)
Async XLA Ops:
  82.1 35.0 %copy-start = (s32[1,256]{1,0:T(1,128)S(1)}, s32[1,256]{1,0:T(1,128)}, u32[]{:S(2)}) copy-start(s32[1,256]{1,0:T(1,128)} %param.9) | copy-start | bytes 3076
